TPU v7x, 32 devices: a whole 2x2x4 slice. The times are simulated.
32 devices in a mesh: energy: 8 (over z, x), tile: 4 (over y, core).
Axes of the slice: x: 2, y: 2, z: 4, core: 2. Of those that a mesh axis runs over, the one named last changes fastest.
Arguments:
- object_tiles: float32 [8, 2, 4, 512, 512], P('energy', None, 'tile'), may hold values from -6 to 6
- probe_wave: float32 [8, 2, 256, 256], P('energy'), may hold values from -6 to 6
- measured: bfloat16 [8, 4, 16, 256, 256], P('energy', 'tile'), may hold values from 0 to 2
- positions: int32 [4, 16, 2], P('tile'), may hold values from 0 to 511, as said below
- materials: float32 [2, 8, 8], replicated, may hold values from -6 to 6
Outputs:
- fitted: float32 [8, 2, 4, 512, 512], P('energy', None, 'tile')
Inputs may be any that keep to these rules, and one draw needn't show every extreme that they name: `positions`: each entry is the corner of a 256 x 256 patch, given inside its tile; in every tile some patch has row corner 512 - 1 and some has column corner 512 - 1.
All inputs are finite; a program needn't handle non-finite values.
Results may differ from a plain program's by a relative error of at most 0.0013.
Values sent between devices are 32-bit elements; how exact they have to be, the bound alone decides.
A program may use at most 64 MiB of HBM per device.

v0:
```python
import math

import jax
import jax.numpy as jnp
from jax import lax
from jax.sharding import PartitionSpec as P

TILE_COLS = 4
FIT_STEPS = 10


amplitude_floor = 0.5


def shifted(value, axis, steps):
    count = lax.axis_size(axis)
    pairs = [(source, (source + steps) % count) for source in range(count)]
    return lax.ppermute(value, axis, pairs)


def fourier_tables(length, direction):
    counter = jnp.arange(length, dtype=jnp.int32)
    products = counter[:, None] * counter[None, :] % length
    angles = 2.0 * math.pi / length * products.astype(jnp.float32)
    cosine = jnp.cos(angles)
    sine = direction * jnp.sin(angles)
    left_table = jnp.concatenate(
        [jnp.concatenate([cosine, sine], 1), jnp.concatenate([-sine, cosine], 1)], 0
    ).astype(jnp.bfloat16)
    right_table = jnp.concatenate(
        [jnp.concatenate([cosine, -sine], 1), jnp.concatenate([sine, cosine], 1)], 0
    ).astype(jnp.bfloat16)
    return (left_table, right_table)


def transform(real_part, imag_part, left_table, right_table):
    length = real_part.shape[0]
    stacked = jnp.concatenate([real_part, imag_part], 0).astype(jnp.bfloat16)
    inner = jnp.dot(left_table, stacked, preferred_element_type=jnp.float32)
    beside = jnp.concatenate([inner[:length], inner[length:]], 1).astype(jnp.bfloat16)
    outer = jnp.dot(beside, right_table, preferred_element_type=jnp.float32) / length
    return (outer[:, :length], outer[:, length:])


def patch_gradient(
    field_real, field_imag, probe_real, probe_imag, amplitude, row_start, col_start, tables
):
    length = probe_real.shape[0]
    piece_real = lax.dynamic_slice(field_real, (row_start, col_start), (length, length))
    piece_imag = lax.dynamic_slice(field_imag, (row_start, col_start), (length, length))
    exit_real = probe_real * piece_real - probe_imag * piece_imag
    exit_imag = probe_real * piece_imag + probe_imag * piece_real
    far_real, far_imag = transform(exit_real, exit_imag, tables[0], tables[1])
    magnitude = jnp.sqrt(far_real * far_real + far_imag * far_imag)
    factor = amplitude.astype(jnp.float32) / jnp.maximum(magnitude, amplitude_floor) - 1.0
    back_real, back_imag = transform(factor * far_real, factor * far_imag, tables[2], tables[3])
    return (
        probe_real * back_real + probe_imag * back_imag,
        probe_real * back_imag - probe_imag * back_real,
    )


def fit_materials(data, materials):
    high = lax.Precision.HIGHEST
    gram = jnp.einsum("rem,ren->mn", materials, materials, precision=high)
    rate = 1.0 / jnp.trace(gram)
    target = jnp.einsum("rem,rep->mp", materials, data, precision=high)

    def descend(number, coefficients):
        slope = jnp.dot(gram, coefficients, precision=high) - target
        return jnp.maximum(coefficients - rate * slope, 0.0)

    return lax.fori_loop(0, FIT_STEPS, descend, jnp.zeros_like(target))


def fitted_spectra(materials, coefficients):
    return jnp.einsum("rem,mp->rep", materials, coefficients, precision=lax.Precision.HIGHEST)


def body(object_tiles, probe_wave, measured, positions, materials):
    own_object = object_tiles[0, :, 0]
    tile_px = own_object.shape[-1]
    length = probe_wave.shape[-1]
    count = measured.shape[2]
    tile_count = lax.axis_size("tile")
    row_step = TILE_COLS % tile_count
    right_strip = shifted(own_object[:, :, :length], "tile", -1)
    widened = jnp.concatenate([own_object, right_strip], 2)
    if row_step:
        lower_strip = shifted(widened[:, :length, :], "tile", -row_step)
    else:
        lower_strip = widened[:, :length, :]
    extended = jnp.concatenate([widened, lower_strip], 1)
    forward = fourier_tables(length, 1.0)
    inverse = fourier_tables(length, -1.0)
    tables = (forward[0], forward[1], inverse[0], inverse[1])
    probe_real = probe_wave[0, 0]
    probe_imag = probe_wave[0, 1]
    own_measured = measured[0, 0]
    corners = positions[0]
    anchor = jnp.zeros((), jnp.int32)

    def accumulate(number, gradient):
        row_start = corners[number, 0]
        col_start = corners[number, 1]
        term_real, term_imag = patch_gradient(
            extended[0],
            extended[1],
            probe_real,
            probe_imag,
            own_measured[number],
            row_start,
            col_start,
            tables,
        )
        current = lax.dynamic_slice(gradient, (anchor, row_start, col_start), (2, length, length))
        return lax.dynamic_update_slice(
            gradient, current + jnp.stack([term_real, term_imag]), (anchor, row_start, col_start)
        )

    gradient = lax.fori_loop(0, count, accumulate, jnp.zeros_like(extended))
    if row_step:
        from_above = shifted(gradient[:, tile_px:, :], "tile", row_step)
    else:
        from_above = gradient[:, tile_px:, :]
    upper = jnp.concatenate(
        [gradient[:, :length, :] + from_above, gradient[:, length:tile_px, :]], 1
    )
    from_left = shifted(upper[:, :, tile_px:], "tile", 1)
    summed = jnp.concatenate([upper[:, :, :length] + from_left, upper[:, :, length:tile_px]], 2)
    peak = jnp.max(probe_real * probe_real + probe_imag * probe_imag)
    updated = own_object + summed / peak
    groups = lax.axis_size("energy")
    pixels = tile_px * tile_px
    group_width = pixels // groups
    outgoing = updated.reshape(2, 1, groups, group_width)
    arrived = lax.all_to_all(outgoing, "energy", split_axis=2, concat_axis=1, tiled=True)
    coefficients = fit_materials(arrived.reshape(2, groups, group_width), materials)
    spectra = fitted_spectra(materials, coefficients).reshape(2, groups, 1, group_width)
    returned = lax.all_to_all(spectra, "energy", split_axis=1, concat_axis=2, tiled=True)
    result = returned.reshape(2, tile_px, tile_px)
    return result.reshape(1, 2, 1, tile_px, tile_px)


def solution(mesh):
    in_specs = (
        P("energy", None, "tile", None, None),
        P("energy", None, None, None),
        P("energy", "tile", None, None, None),
        P("tile", None, None),
        P(),
    )
    out_specs = P("energy", None, "tile", None, None)
    return jax.shard_map(body, mesh=mesh, in_specs=in_specs, out_specs=out_specs, check_vma=False)
```

profile of v0, /device:TPU:0, one launch (start us, length us, event | category | flops | bytes accessed | tf_op | source)
XLA Modules:
  0.0 485.5 jit_solution(13260882390065137983)
XLA Ops:
  0.0 2.3 slice.152
  2.3 2.4 collective-permute-start
  8.8 8.5 %collective-permute-done = f32[2,512,256]{2,1,0:T(8,128)} collective-permute-done((f32[2,512,256]{2,1,0:T(8,128)}, f32[2,512,256]{2,1,0:T(8,128)}, u32[]{:S(2)}, u32[]{:S(2)}) %collective-permute-start) | collective-permute-done | bytes 1048608 | tf_op jit(solution)/shard_map/ppermute | solution.py:18
  17.4 3.9 fusion.30
  21.2 2.5 broadcast_in_dim.12
  23.7 301.3 %while.26 = (s32[]{:T(128)}, f32[2,768,768]{2,1,0:T(8,128)}, s32[16,2]{0,1:T(2,128)S(1)}, bf16[16,256,256]{2,1,0:T(8,128)(2,1)}, f32[2,768,768]{2,1,0:T(8,128)},...) while((s32[]{:T(128)}, f32[2,768,768]{2,1,0:T(8,128)}, ...), condition=%wide.region_1.2_spmd, body=%wide.region_0.1_spmd.sunk | while | flops 541392896 | bytes 21627124 | solution.py:121
  28.1 2.7 fusion.88
  31.0 1.4 fusion.90
  36.0 6.5 %dynamic_update_slice.11 = f32[2,768,768]{2,1,0:T(8,128)} dynamic-update-slice(f32[2,768,768]{2,1,0:T(8,128)} %get-tuple-element.519, f32[2,256,256]{2,1,0:T(8,128)S(1)} %maximum_add_fusion.2, s32[]{:T(128)} %constant.115.clone.1..sunk, s32[]{:T(128)S(6)} %select_n.102, s32[]{:T(128)S(6)} %select_n.103) | dynamic-update-slice | bytes 1048580 | tf_op jit(solution)/shard_map/while/body/eval_jaxpr/dynamic_update_slice | solution.py:117
  46.9 2.7 fusion.88
  49.9 1.4 fusion.90
  54.8 6.0 %dynamic_update_slice.11 = f32[2,768,768]{2,1,0:T(8,128)} dynamic-update-slice(f32[2,768,768]{2,1,0:T(8,128)} %get-tuple-element.519, f32[2,256,256]{2,1,0:T(8,128)S(1)} %maximum_add_fusion.2, s32[]{:T(128)} %constant.115.clone.1..sunk, s32[]{:T(128)S(6)} %select_n.102, s32[]{:T(128)S(6)} %select_n.103) | dynamic-update-slice | bytes 1048580 | tf_op jit(solution)/shard_map/while/body/eval_jaxpr/dynamic_update_slice | solution.py:117
  65.2 2.7 fusion.88
  68.2 1.4 fusion.90
  73.2 6.2 %dynamic_update_slice.11 = f32[2,768,768]{2,1,0:T(8,128)} dynamic-update-slice(f32[2,768,768]{2,1,0:T(8,128)} %get-tuple-element.519, f32[2,256,256]{2,1,0:T(8,128)S(1)} %maximum_add_fusion.2, s32[]{:T(128)} %constant.115.clone.1..sunk, s32[]{:T(128)S(6)} %select_n.102, s32[]{:T(128)S(6)} %select_n.103) | dynamic-update-slice | bytes 1048580 | tf_op jit(solution)/shard_map/while/body/eval_jaxpr/dynamic_update_slice | solution.py:117
  83.8 2.7 fusion.88
  86.7 1.4 fusion.90
  91.7 6.5 %dynamic_update_slice.11 = f32[2,768,768]{2,1,0:T(8,128)} dynamic-update-slice(f32[2,768,768]{2,1,0:T(8,128)} %get-tuple-element.519, f32[2,256,256]{2,1,0:T(8,128)S(1)} %maximum_add_fusion.2, s32[]{:T(128)} %constant.115.clone.1..sunk, s32[]{:T(128)S(6)} %select_n.102, s32[]{:T(128)S(6)} %select_n.103) | dynamic-update-slice | bytes 1048580 | tf_op jit(solution)/shard_map/while/body/eval_jaxpr/dynamic_update_slice | solution.py:117
  102.6 2.7 fusion.88
  105.5 1.4 fusion.90
  110.5 6.8 %dynamic_update_slice.11 = f32[2,768,768]{2,1,0:T(8,128)} dynamic-update-slice(f32[2,768,768]{2,1,0:T(8,128)} %get-tuple-element.519, f32[2,256,256]{2,1,0:T(8,128)S(1)} %maximum_add_fusion.2, s32[]{:T(128)} %constant.115.clone.1..sunk, s32[]{:T(128)S(6)} %select_n.102, s32[]{:T(128)S(6)} %select_n.103) | dynamic-update-slice | bytes 1048580 | tf_op jit(solution)/shard_map/while/body/eval_jaxpr/dynamic_update_slice | solution.py:117
  121.7 2.7 fusion.88
  129.6 6.8 %dynamic_update_slice.11 = f32[2,768,768]{2,1,0:T(8,128)} dynamic-update-slice(f32[2,768,768]{2,1,0:T(8,128)} %get-tuple-element.519, f32[2,256,256]{2,1,0:T(8,128)S(1)} %maximum_add_fusion.2, s32[]{:T(128)} %constant.115.clone.1..sunk, s32[]{:T(128)S(6)} %select_n.102, s32[]{:T(128)S(6)} %select_n.103) | dynamic-update-slice | bytes 1048580 | tf_op jit(solution)/shard_map/while/body/eval_jaxpr/dynamic_update_slice | solution.py:117
  140.8 2.7 fusion.88
  143.8 1.4 fusion.90
  148.8 6.8 %dynamic_update_slice.11 = f32[2,768,768]{2,1,0:T(8,128)} dynamic-update-slice(f32[2,768,768]{2,1,0:T(8,128)} %get-tuple-element.519, f32[2,256,256]{2,1,0:T(8,128)S(1)} %maximum_add_fusion.2, s32[]{:T(128)} %constant.115.clone.1..sunk, s32[]{:T(128)S(6)} %select_n.102, s32[]{:T(128)S(6)} %select_n.103) | dynamic-update-slice | bytes 1048580 | tf_op jit(solution)/shard_map/while/body/eval_jaxpr/dynamic_update_slice | solution.py:117
  159.9 2.7 fusion.88
  167.8 6.8 %dynamic_update_slice.11 = f32[2,768,768]{2,1,0:T(8,128)} dynamic-update-slice(f32[2,768,768]{2,1,0:T(8,128)} %get-tuple-element.519, f32[2,256,256]{2,1,0:T(8,128)S(1)} %maximum_add_fusion.2, s32[]{:T(128)} %constant.115.clone.1..sunk, s32[]{:T(128)S(6)} %select_n.102, s32[]{:T(128)S(6)} %select_n.103) | dynamic-update-slice | bytes 1048580 | tf_op jit(solution)/shard_map/while/body/eval_jaxpr/dynamic_update_slice | solution.py:117
  179.1 2.7 fusion.88
  187.0 6.8 %dynamic_update_slice.11 = f32[2,768,768]{2,1,0:T(8,128)} dynamic-update-slice(f32[2,768,768]{2,1,0:T(8,128)} %get-tuple-element.519, f32[2,256,256]{2,1,0:T(8,128)S(1)} %maximum_add_fusion.2, s32[]{:T(128)} %constant.115.clone.1..sunk, s32[]{:T(128)S(6)} %select_n.102, s32[]{:T(128)S(6)} %select_n.103) | dynamic-update-slice | bytes 1048580 | tf_op jit(solution)/shard_map/while/body/eval_jaxpr/dynamic_update_slice | solution.py:117
  198.1 2.7 fusion.88
  201.0 1.4 fusion.90
  206.0 6.3 %dynamic_update_slice.11 = f32[2,768,768]{2,1,0:T(8,128)} dynamic-update-slice(f32[2,768,768]{2,1,0:T(8,128)} %get-tuple-element.519, f32[2,256,256]{2,1,0:T(8,128)S(1)} %maximum_add_fusion.2, s32[]{:T(128)} %constant.115.clone.1..sunk, s32[]{:T(128)S(6)} %select_n.102, s32[]{:T(128)S(6)} %select_n.103) | dynamic-update-slice | bytes 1048580 | tf_op jit(solution)/shard_map/while/body/eval_jaxpr/dynamic_update_slice | solution.py:117
  216.7 2.7 fusion.88
  224.6 6.4 %dynamic_update_slice.11 = f32[2,768,768]{2,1,0:T(8,128)} dynamic-update-slice(f32[2,768,768]{2,1,0:T(8,128)} %get-tuple-element.519, f32[2,256,256]{2,1,0:T(8,128)S(1)} %maximum_add_fusion.2, s32[]{:T(128)} %constant.115.clone.1..sunk, s32[]{:T(128)S(6)} %select_n.102, s32[]{:T(128)S(6)} %select_n.103) | dynamic-update-slice | bytes 1048580 | tf_op jit(solution)/shard_map/while/body/eval_jaxpr/dynamic_update_slice | solution.py:117
  235.4 2.7 fusion.88
  243.3 6.7 %dynamic_update_slice.11 = f32[2,768,768]{2,1,0:T(8,128)} dynamic-update-slice(f32[2,768,768]{2,1,0:T(8,128)} %get-tuple-element.519, f32[2,256,256]{2,1,0:T(8,128)S(1)} %maximum_add_fusion.2, s32[]{:T(128)} %constant.115.clone.1..sunk, s32[]{:T(128)S(6)} %select_n.102, s32[]{:T(128)S(6)} %select_n.103) | dynamic-update-slice | bytes 1048580 | tf_op jit(solution)/shard_map/while/body/eval_jaxpr/dynamic_update_slice | solution.py:117
  254.4 2.7 fusion.88
  262.3 6.5 %dynamic_update_slice.11 = f32[2,768,768]{2,1,0:T(8,128)} dynamic-update-slice(f32[2,768,768]{2,1,0:T(8,128)} %get-tuple-element.519, f32[2,256,256]{2,1,0:T(8,128)S(1)} %maximum_add_fusion.2, s32[]{:T(128)} %constant.115.clone.1..sunk, s32[]{:T(128)S(6)} %select_n.102, s32[]{:T(128)S(6)} %select_n.103) | dynamic-update-slice | bytes 1048580 | tf_op jit(solution)/shard_map/while/body/eval_jaxpr/dynamic_update_slice | solution.py:117
  273.2 2.7 fusion.88
  276.1 1.4 fusion.90
  281.1 6.6 %dynamic_update_slice.11 = f32[2,768,768]{2,1,0:T(8,128)} dynamic-update-slice(f32[2,768,768]{2,1,0:T(8,128)} %get-tuple-element.519, f32[2,256,256]{2,1,0:T(8,128)S(1)} %maximum_add_fusion.2, s32[]{:T(128)} %constant.115.clone.1..sunk, s32[]{:T(128)S(6)} %select_n.102, s32[]{:T(128)S(6)} %select_n.103) | dynamic-update-slice | bytes 1048580 | tf_op jit(solution)/shard_map/while/body/eval_jaxpr/dynamic_update_slice | solution.py:117
  292.1 2.7 fusion.88
  300.0 6.4 %dynamic_update_slice.11 = f32[2,768,768]{2,1,0:T(8,128)} dynamic-update-slice(f32[2,768,768]{2,1,0:T(8,128)} %get-tuple-element.519, f32[2,256,256]{2,1,0:T(8,128)S(1)} %maximum_add_fusion.2, s32[]{:T(128)} %constant.115.clone.1..sunk, s32[]{:T(128)S(6)} %select_n.102, s32[]{:T(128)S(6)} %select_n.103) | dynamic-update-slice | bytes 1048580 | tf_op jit(solution)/shard_map/while/body/eval_jaxpr/dynamic_update_slice | solution.py:117
  310.8 2.7 fusion.88
  313.7 1.4 fusion.90
  318.7 6.3 %dynamic_update_slice.11 = f32[2,768,768]{2,1,0:T(8,128)} dynamic-update-slice(f32[2,768,768]{2,1,0:T(8,128)} %get-tuple-element.519, f32[2,256,256]{2,1,0:T(8,128)S(1)} %maximum_add_fusion.2, s32[]{:T(128)} %constant.115.clone.1..sunk, s32[]{:T(128)S(6)} %select_n.102, s32[]{:T(128)S(6)} %select_n.103) | dynamic-update-slice | bytes 1048580 | tf_op jit(solution)/shard_map/while/body/eval_jaxpr/dynamic_update_slice | solution.py:117
  325.0 2.6 slice_add_fusion
  330.0 2.7 squeeze.51
  333.4 11.6 %collective-permute-done.1 = f32[2,512,256]{2,1,0:T(8,128)} collective-permute-done((f32[2,512,256]{2,1,0:T(8,128)}, f32[2,512,256]{2,1,0:T(8,128)}, u32[]{:S(2)}, u32[]{:S(2)}) %collective-permute-start.1) | collective-permute-done | bytes 1048608 | tf_op jit(solution)/shard_map/ppermute | solution.py:18
  345.0 1.5 fusion.37
  346.5 2.2 fusion.32
  348.7 2.7 div.42
  351.5 2.4 add.166
  353.9 2.9 copy.11
  356.8 5.8 %all-to-all-start = ((f32[2,1,8,32768]{3,0,1,2:T(2,128)}), f32[2,1,8,32768]{3,0,1,2:T(2,128)}, u32[]{:S(2)}, u32[]{:S(2)}) async-start(f32[2,1,8,32768]{3,0,1,2:T(2,128)} %copy.11), calls=%async_computation | async-start | bytes 4194304 | tf_op jit(solution)/shard_map/all_to_all | solution.py:137
  364.2 44.7 %all-to-all-done = f32[2,1,8,32768]{3,0,1,2:T(2,128)} async-done(((f32[2,1,8,32768]{3,0,1,2:T(2,128)}), f32[2,1,8,32768]{3,0,1,2:T(2,128)}, u32[]{:S(2)}, u32[]{:S(2)}) %all-to-all-start) | async-done | bytes 2097184 | tf_op jit(solution)/shard_map/all_to_all | solution.py:137
  408.9 3.9 convolution_bitcast_fusion.1
  412.8 12.5 %while.27 = (s32[]{:T(128)}, f32[8,32768]{1,0:T(8,128)S(1)}, f32[]{:T(128)}, f32[8,8]{1,0:T(8,128)S(1)}, f32[8,32768]{1,0:T(8,128)S(1)}, /*index=5*/s32[]{:T(128)}, s32[]{:T(128)}) while((s32[]{:T(128)}, f32[8,32768]{1,0:T(8,128)S(1)}, f32[]{:T(128)}, f32[8,8]{1,0:T(8,128)S(1)}, f32[8,32768]{1,0:T(8,128)S(1)}, ...), condition=%wide.region_5.6_spmd.clone, body=%wide.region_4.5_spmd.clone.sunk | while | flops 26738692 | bytes 5243227 | solution.py:73
  425.3 1.8 convolution_bitcast_fusion
  427.1 1.6 copy.14
  428.7 51.5 %all_to_all.8 = f32[2,8,1,32768]{3,0,2,1:T(2,128)S(1)} all-to-all(f32[2,8,1,32768]{3,0,2,1:T(2,128)S(1)} %copy.14), channel_id=1, replica_groups=mesh['energy'=8,'tile'=4] {'energy'}, dimensions={1} | all-to-all | bytes 4194304 | tf_op jit(solution)/shard_map/all_to_all | solution.py:140
  480.2 2.6 copy.15
  482.8 2.7 reshape_reshape.3
  (209 shorter events, 99.7 us)
Async XLA Ops:
  0.0 362.6 %copy-start = (f32[2,8,8]{2,1,0:T(8,128)S(1)}, f32[2,8,8]{2,1,0:T(8,128)}, u32[]{:S(2)}) copy-start(f32[2,8,8]{2,1,0:T(8,128)} %param.13) | copy-start | bytes 1540
  2.3 6.5 %copy-start.4 = (f32[1,2,256,256]{3,2,1,0:T(8,128)S(1)}, f32[1,2,256,256]{3,2,1,0:T(8,128)}, u32[]{:S(2)}) copy-start(f32[1,2,256,256]{3,2,1,0:T(8,128)} %param.10) | copy-start | bytes 1572868
  2.3 15.1 %collective-permute-start = (f32[2,512,256]{2,1,0:T(8,128)}, f32[2,512,256]{2,1,0:T(8,128)}, u32[]{:S(2)}, u32[]{:S(2)}) collective-permute-start(f32[2,512,256]{2,1,0:T(8,128)} %slice.152), channel_id=1, source_target_pairs={{0,3},{1,0},{2,1},{3,2},{4,7},{5,4},{6,5},{7,6},{8,11},{9,8},{10,9... | collective-permute-start | bytes 3145736 | tf_op jit(solution)/shard_map/ppermute | solution.py:18
  6.7 10.6 %copy-start.3 = (f32[1,2,1,512,512]{4,3,2,1,0:T(8,128)S(1)}, f32[1,2,1,512,512]{4,3,2,1,0:T(8,128)}, u32[]{:S(2)}) copy-start(f32[1,2,1,512,512]{4,3,2,1,0:T(8,128)} %param.9) | copy-start | bytes 6291460
  21.2 2.5 copy-start.5
  327.6 1.5 copy-start.1
  329.1 15.8 %collective-permute-start.1 = (f32[2,512,256]{2,1,0:T(8,128)}, f32[2,512,256]{2,1,0:T(8,128)}, u32[]{:S(2)}, u32[]{:S(2)}) collective-permute-start(f32[2,512,256]{2,1,0:T(8,128)} %fusion.35), channel_id=1, source_target_pairs={{0,1},{1,2},{2,3},{3,0},{4,5},{5,6},{6,7},{7,4},{8,9},{9,10},{10,1... | collective-permute-start | bytes 3145736 | tf_op jit(solution)/shard_map/ppermute | solution.py:18
  333.4 13.2 %copy-start.2 = (f32[2,256,768]{2,1,0:T(8,128)S(1)}, f32[2,256,768]{2,1,0:T(8,128)}, u32[]{:S(2)}) copy-start(f32[2,256,768]{2,1,0:T(8,128)} %copy-done.1) | copy-start | bytes 4718596
  356.8 52.0 %all-to-all-start = ((f32[2,1,8,32768]{3,0,1,2:T(2,128)}), f32[2,1,8,32768]{3,0,1,2:T(2,128)}, u32[]{:S(2)}, u32[]{:S(2)}) async-start(f32[2,1,8,32768]{3,0,1,2:T(2,128)} %copy.11), calls=%async_computation | async-start | bytes 4194304 | tf_op jit(solution)/shard_map/all_to_all | solution.py:137
where the time goes:
time: 492 us; the launch traced here: 486 us
  local copies, waits for them, and re-layouts  179 us (36%)
  waiting for transfers between devices  64.8 us (13%)
  other arithmetic  62.6 us (13%)
  loops' own time  62.1 us (13%)
  matrix products  56 us (11%)
  blocking collectives  51.5 us (10%)
  starting transfers between devices  9.06 us (2%)
    dynamic_update_slice x16, local copies, waits for them, and re-layouts, accumulate(): lax.dynamic_update_slice(gradient, current + jnp.stack([term_real, term_i...  105 us
    another operation x1, loops' own time, body(): gradient = lax.fori_loop(0, count, accumulate, jnp.zeros_like(extended))  61.8 us
    all_to_all x1, blocking collectives, body(): lax.all_to_all(spectra, 'energy', split_axis=1, concat_axis=2, tiled=True)  51.5 us
    all_to_all x1, waiting for transfers between devices, body(): lax.all_to_all(outgoing, 'energy', split_axis=2, concat_axis=1, tiled=True)  44.7 us
    slice x16, local copies, waits for them, and re-layouts, accumulate(): extended[0]  42.9 us
    dot_general x32, matrix products, transform(): inner = jnp.dot(left_table, stacked, preferred_element_type=jnp.float32)  27.8 us
    another operation x35, other arithmetic  23.9 us
    add x16, other arithmetic, accumulate(): current + jnp.stack([term_real, term_imag])  22 us
  transfers between devices with their start and end apart: 3, of which 3 were waited for; matrix products, arithmetic and copies ran while one was open for 2% of the time, Pallas kernels for 0%

commit v1 on v0

v1 whole, which is shorter than its diff:
```python
import functools
import math

import jax
import jax.numpy as jnp
import numpy as np
from jax import lax
from jax.experimental import pallas as pl
from jax.experimental.pallas import tpu as pltpu
from jax.sharding import PartitionSpec as P

TILE_COLS = 4
FIT_STEPS = 10
LANES = 128


amplitude_floor = 0.5


def shifted(value, axis, steps):
    count = lax.axis_size(axis)
    pairs = [(source, (source + steps) % count) for source in range(count)]
    return lax.ppermute(value, axis, pairs)


def fourier_parts(length):
    counter = np.arange(length, dtype=np.int64)
    angles = 2.0 * math.pi / length * (counter[:, None] * counter[None, :] % length)
    return (
        jnp.asarray(np.cos(angles), jnp.float32).astype(jnp.bfloat16),
        jnp.asarray(np.sin(angles), jnp.float32).astype(jnp.bfloat16),
    )


def joined(top_left, top_right, bottom_left, bottom_right):
    return jnp.concatenate(
        [
            jnp.concatenate([top_left, top_right], 1),
            jnp.concatenate([bottom_left, bottom_right], 1),
        ],
        0,
    )


def transform(real_part, imag_part, left_ref, right_ref):
    length = real_part.shape[0]
    stacked = jnp.concatenate([real_part.astype(jnp.bfloat16), imag_part.astype(jnp.bfloat16)], 0)
    inner = jnp.dot(left_ref[...], stacked, preferred_element_type=jnp.float32)
    inner = inner.astype(jnp.bfloat16)
    beside = jnp.concatenate([inner[:length], inner[length:]], 1)
    outer = jnp.dot(beside, right_ref[...], preferred_element_type=jnp.float32) * (1.0 / length)
    return outer[:, :length], outer[:, length:]


def window(ref, part, row, block, shift, length):
    lane = lax.broadcasted_iota(jnp.int32, (length, LANES), 1)
    back = lax.rem(LANES - shift, LANES)
    tiles = [
        pltpu.roll(ref[part, block + at, pl.ds(row, length), :], back, 1)
        for at in range(length // LANES + 1)
    ]
    keep = lane < LANES - shift
    return jnp.concatenate(
        [jnp.where(keep, one, other) for one, other in zip(tiles[:-1], tiles[1:])], 1
    )


def add_window(ref, part, row, block, shift, term):
    length = term.shape[0]
    lane = lax.broadcasted_iota(jnp.int32, (length, LANES), 1)
    tiles = [pltpu.roll(term[:, at : at + LANES], shift, 1) for at in range(0, length, LANES)]
    keep = lane >= shift
    zero = jnp.zeros_like(tiles[0])
    for at, (one, other) in enumerate(zip(tiles + [zero], [zero] + tiles)):
        place = (part, block + at, pl.ds(row, length), slice(None))
        ref[place] = ref[place] + jnp.where(keep, one, other)


def patch_kernel(
    fold,
    corners_ref,
    object_ref,
    right_ref,
    lower_ref,
    probe_ref,
    measured_ref,
    cosine_ref,
    sine_ref,
    main_out,
    side_out,
    below_out,
    field,
    gradient,
    tables,
    sems,
):
    tile_px = object_ref.shape[-1]
    length = probe_ref.shape[-1]
    count = measured_ref.shape[0]
    blocks = tile_px // LANES
    top = pl.ds(0, tile_px)
    bottom = pl.ds(tile_px, length)
    moves = []
    for block in range(blocks + length // LANES):
        ref, at = (object_ref, block) if block < blocks else (right_ref, block - blocks)
        columns = pl.ds(at * LANES, LANES)
        moves.append((ref.at[:, :, columns], field.at[:, block, top, :]))
        if fold:
            source = ref.at[:, pl.ds(0, length), columns]
        else:
            source = lower_ref.at[:, :, pl.ds(block * LANES, LANES)]
        moves.append((source, field.at[:, block, bottom, :]))
    copies = [
        pltpu.make_async_copy(source, target, sems.at[number])
        for number, (source, target) in enumerate(moves)
    ]
    for copy in copies:
        copy.start()
    cosine = cosine_ref[...]
    sine = sine_ref[...]
    tables[0] = joined(cosine, sine, -sine, cosine)
    tables[1] = joined(cosine, -sine, sine, cosine)
    gradient[...] = jnp.zeros_like(gradient)
    for copy in copies:
        copy.wait()

    def step(number, carry):
        row = corners_ref[number, 0]
        col = corners_ref[number, 1]
        block = col // LANES
        shift = col - block * LANES
        piece_real = window(field, 0, row, block, shift, length)
        piece_imag = window(field, 1, row, block, shift, length)
        probe_real = probe_ref[0]
        probe_imag = probe_ref[1]
        exit_real = probe_real * piece_real - probe_imag * piece_imag
        exit_imag = probe_real * piece_imag + probe_imag * piece_real
        far_real, far_imag = transform(exit_real, exit_imag, tables.at[0], tables.at[1])
        square = far_real * far_real + far_imag * far_imag
        scale = lax.rsqrt(jnp.maximum(square, amplitude_floor * amplitude_floor))
        factor = measured_ref[number].astype(jnp.float32) * scale - 1.0
        back_real, back_imag = transform(
            factor * far_real, factor * far_imag, tables.at[1], tables.at[0]
        )
        probe_real = probe_ref[0]
        probe_imag = probe_ref[1]
        add_window(
            gradient, 0, row, block, shift, probe_real * back_real + probe_imag * back_imag
        )
        add_window(
            gradient, 1, row, block, shift, probe_real * back_imag - probe_imag * back_real
        )
        return carry

    lax.fori_loop(0, count, step, 0)
    peak = jnp.max(probe_ref[0] * probe_ref[0] + probe_ref[1] * probe_ref[1])
    rows = 64

    def finish(wrapped, number, carry):
        place = (pl.ds(pl.multiple_of(number * rows, rows), rows), slice(None))
        beyond = pl.ds(pl.multiple_of(tile_px + number * rows, rows), rows)
        for part in range(2):
            for block in range(blocks + length // LANES):
                total = gradient[(part, block) + place]
                if wrapped:
                    total = total + gradient[part, block, beyond, :]
                share = total / peak
                if block < blocks:
                    columns = slice(block * LANES, (block + 1) * LANES)
                    main_out[part, place[0], columns] = field[(part, block) + place] + share
                else:
                    columns = slice((block - blocks) * LANES, (block - blocks + 1) * LANES)
                    side_out[part, place[0], columns] = share
        return carry

    lax.fori_loop(0, length // rows, functools.partial(finish, fold), 0)
    lax.fori_loop(length // rows, tile_px // rows, functools.partial(finish, False), 0)
    if fold:
        below_out[...] = jnp.zeros_like(below_out)
    else:
        for block in range(blocks + length // LANES):
            columns = slice(block * LANES, (block + 1) * LANES)
            below_out[:, :, columns] = gradient[:, block, tile_px:, :] / peak


def patch_update(own_object, right_strip, lower_strip, probe, measured, corners, fold):
    tile_px = own_object.shape[-1]
    length = probe.shape[-1]
    count = measured.shape[0]
    width = tile_px + length
    cosine, sine = fourier_parts(length)
    below = (2, 8, LANES) if fold else (2, length, width)
    vmem = pl.BlockSpec(memory_space=pltpu.VMEM)
    anywhere = pl.BlockSpec(memory_space=pl.ANY)
    return pl.pallas_call(
        functools.partial(patch_kernel, fold),
        out_shape=(
            jax.ShapeDtypeStruct((2, tile_px, tile_px), jnp.float32),
            jax.ShapeDtypeStruct((2, tile_px, length), jnp.float32),
            jax.ShapeDtypeStruct(below, jnp.float32),
        ),
        in_specs=[
            pl.BlockSpec(memory_space=pltpu.SMEM),
            anywhere,
            anywhere,
            anywhere,
            vmem,
            vmem,
            vmem,
            vmem,
        ],
        out_specs=(vmem, vmem, vmem),
        scratch_shapes=[
            pltpu.VMEM((2, width // LANES, width, LANES), jnp.float32),
            pltpu.VMEM((2, width // LANES, width, LANES), jnp.float32),
            pltpu.VMEM((2, 2 * length, 2 * length), jnp.bfloat16),
            pltpu.SemaphoreType.DMA((2 * (width // LANES),)),
        ],
        compiler_params=pltpu.CompilerParams(vmem_limit_bytes=48 * 1024 * 1024),
        cost_estimate=pl.CostEstimate(
            flops=64 * count * length**3, bytes_accessed=16 * tile_px * tile_px, transcendentals=0
        ),
        name="patches",
    )(corners, own_object, right_strip, lower_strip, probe, measured, cosine, sine)


def fit_scalars(materials_ref, energies, kinds):
    spectra = [
        [materials_ref[(part * energies + energy) * kinds + kind] for kind in range(kinds)]
        for part in range(2)
        for energy in range(energies)
    ]
    gram = [[None] * kinds for _ in range(kinds)]
    for one in range(kinds):
        for other in range(one, kinds):
            total = spectra[0][one] * spectra[0][other]
            for row in spectra[1:]:
                total = total + row[one] * row[other]
            gram[one][other] = total
            gram[other][one] = total
    trace = gram[0][0]
    for one in range(1, kinds):
        trace = trace + gram[one][one]
    return gram, trace


def fit_kernel(materials_ref, data_ref, out_ref, step_ref):
    energies, rows, width = data_ref.shape[1:]
    kinds = materials_ref.shape[0] // (2 * energies)
    gram, trace = fit_scalars(materials_ref, energies, kinds)
    rate = 1.0 / trace
    for one in range(kinds):
        for other in range(kinds):
            unit = 1.0 if one == other else 0.0
            step_ref[one * kinds + other] = unit - rate * gram[one][other]
    tall, wide = 8, 256
    across = width // wide
    pairs = [(part, energy) for part in range(2) for energy in range(energies)]

    def chunk(number, carry):
        row = pl.multiple_of(number // across * tall, tall)
        col = pl.multiple_of(number % across * wide, wide)
        place = (pl.ds(row, tall), pl.ds(col, wide))
        target = [None] * kinds
        for part, energy in pairs:
            plane = data_ref[(part, energy) + place]
            for kind in range(kinds):
                term = materials_ref[(part * energies + energy) * kinds + kind] * plane
                target[kind] = term if target[kind] is None else target[kind] + term
        target = [rate * value for value in target]
        current = [jnp.maximum(value, 0.0) for value in target]

        def descend(turn, current):
            following = []
            for one in range(kinds):
                total = target[one]
                for other in range(kinds):
                    total = total + step_ref[one * kinds + other] * current[other]
                following.append(jnp.maximum(total, 0.0))
            return following

        current = lax.fori_loop(1, FIT_STEPS, descend, current)
        for part, energy in pairs:
            total = None
            for kind in range(kinds):
                term = materials_ref[(part * energies + energy) * kinds + kind] * current[kind]
                total = term if total is None else total + term
            out_ref[(part, energy) + place] = total
        return carry

    lax.fori_loop(0, rows // tall * across, chunk, 0)


def fit_spectra(data, materials):
    kinds = materials.shape[-1]
    vmem = pl.BlockSpec(memory_space=pltpu.VMEM)
    return pl.pallas_call(
        fit_kernel,
        out_shape=jax.ShapeDtypeStruct(data.shape, jnp.float32),
        in_specs=[pl.BlockSpec(memory_space=pltpu.SMEM), vmem],
        out_specs=vmem,
        scratch_shapes=[pltpu.SMEM((kinds * kinds,), jnp.float32)],
        name="fit",
    )(materials.reshape(-1), data)


def body(object_tiles, probe_wave, measured, positions, materials):
    own_object = object_tiles[0, :, 0]
    tile_px = own_object.shape[-1]
    length = probe_wave.shape[-1]
    tile_count = lax.axis_size("tile")
    row_step = TILE_COLS % tile_count
    fold = row_step == 0
    right_strip = shifted(own_object[:, :, :length], "tile", -1)
    if fold:
        lower_strip = jnp.zeros((2, 8, LANES), jnp.float32)
    else:
        widened = jnp.concatenate([own_object[:, :length], right_strip[:, :length]], 2)
        lower_strip = shifted(widened, "tile", -row_step)
    main, side, below = patch_update(
        own_object, right_strip, lower_strip, probe_wave[0], measured[0, 0], positions[0], fold
    )
    if not fold:
        from_above = shifted(below, "tile", row_step)
        main = main.at[:, :length, :].add(from_above[:, :, :tile_px])
        side = side.at[:, :length, :].add(from_above[:, :, tile_px:])
    from_left = shifted(side, "tile", 1)
    updated = jnp.concatenate([main[:, :, :length] + from_left, main[:, :, length:]], 2)
    groups = lax.axis_size("energy")
    group_rows = tile_px // groups
    outgoing = updated.reshape(2, groups, group_rows, tile_px)
    arrived = lax.all_to_all(outgoing, "energy", split_axis=1, concat_axis=1, tiled=True)
    spectra = fit_spectra(arrived, materials)
    returned = lax.all_to_all(spectra, "energy", split_axis=1, concat_axis=1, tiled=True)
    return returned.reshape(1, 2, 1, tile_px, tile_px)


def solution(mesh):
    in_specs = (
        P("energy", None, "tile", None, None),
        P("energy", None, None, None),
        P("energy", "tile", None, None, None),
        P("tile", None, None),
        P(),
    )
    out_specs = P("energy", None, "tile", None, None)
    return jax.shard_map(body, mesh=mesh, in_specs=in_specs, out_specs=out_specs, check_vma=False)
```

time: 492 us -> 190 us (0.39); the launches traced: 486 us -> 189 us
  local copies, waits for them, and re-layouts: 179 us -> 8.57 us
  loops' own time: 62.1 us -> 0 us
  other arithmetic: 62.6 us -> 0.64 us
  matrix products: 56 us -> 0 us
  Pallas kernels: 0 us -> 47.3 us
  waiting for transfers between devices: 64.8 us -> 71.8 us
    dynamic_update_slice x16 -> x0, local copies, waits for them, and re-layouts: 105 us -> none  [accumulate(): lax.dynamic_update_slice(gradient, current + jnp.stack([term_real, term_i...]
    another operation x2 -> x0, loops' own time: 62.1 us -> none  [the longest x1 61.8 us: body(): gradient = lax.fori_loop(0, count, accumulate, jnp.zeros_like(extended))]
    dot_general x77 -> x0, matrix products: 56 us -> none  [the longest x32 27.8 us: transform(): inner = jnp.dot(left_table, stacked, preferred_element_type=jnp.float32)]
    pallas_call x0 -> x2, Pallas kernels: none -> 47.3 us  [the longest x1 33.1 us: patch_update(): pl.pallas_call(functools.partial(patch_kernel, fold), out_shape=(jax.Shap...]
    slice x48 -> x0, local copies, waits for them, and re-layouts: 43.5 us -> none  [the longest x16 42.9 us: accumulate(): extended[0]]
    add x19 -> x1, other arithmetic: 28.7 us -> 0.33 us  [body(): main[:, :, :length] + from_left]
    another operation x51 -> x0, other arithmetic: 25.1 us -> none
    dynamic_slice x16 -> x0, local copies, waits for them, and re-layouts: 9.48 us -> none  [accumulate(): col_start = corners[number, 1]]
  transfers between devices with their start and end apart: 3 -> 3, of which waited for: 3 -> 3; matrix products, arithmetic and copies ran while one was open for 2% -> 0% of each run, Pallas kernels for 0% -> 0%
where the time goes in v1:
time: 190 us; the launch traced here: 189 us
  waiting for transfers between devices  71.8 us (38%)
  blocking collectives  51.7 us (27%)
  Pallas kernels  47.3 us (25%)
  starting transfers between devices  9.31 us (5%)
  local copies, waits for them, and re-layouts  8.57 us (5%)
    all_to_all x1, blocking collectives, body(): lax.all_to_all(spectra, 'energy', split_axis=1, concat_axis=1, tiled=True)  51.7 us
    all_to_all x1, waiting for transfers between devices, body(): lax.all_to_all(outgoing, 'energy', split_axis=1, concat_axis=1, tiled=True)  46 us
    pallas_call x1, Pallas kernels, patch_update(): pl.pallas_call(functools.partial(patch_kernel, fold), out_shape=(jax.Shap...  33.1 us
    ppermute x2, waiting for transfers between devices, shifted(): return lax.ppermute(value, axis, pairs)  25.8 us
    pallas_call x1, Pallas kernels, fit_spectra(): pl.pallas_call(fit_kernel, out_shape=jax.ShapeDtypeStruct(data.shape, jnp...  14.1 us
    all_to_all x1, starting transfers between devices, body(): lax.all_to_all(outgoing, 'energy', split_axis=1, concat_axis=1, tiled=True)  5.94 us
  transfers between devices with their start and end apart: 3, of which 3 were waited for; matrix products, arithmetic and copies ran while one was open for 0% of the time, Pallas kernels for 0%

profile of v1, /device:TPU:0, one launch (start us, length us, event | category | flops | bytes accessed | tf_op | source)
XLA Modules:
  0.0 189.3 jit_solution(18206370278161091234)
XLA Ops:
  0.0 0.0 copy-start.1
  0.0 0.0 copy-start.2
  0.0 0.0 copy-start.4
  0.0 0.0 copy-start
  0.0 1.4 slice.12
  1.4 2.5 %collective-permute-start = (f32[2,512,256]{2,1,0:T(8,128)S(1)}, f32[2,512,256]{2,1,0:T(8,128)S(1)}, u32[]{:S(2)}, u32[]{:S(2)}) collective-permute-start(f32[2,512,256]{2,1,0:T(8,128)S(1)} %slice.12), channel_id=1, source_target_pairs={{0,3},{1,0},{2,1},{3,2},{4,7},{5,4},{6,5},{7,6},{8,11},{9,8},{10,9... | collective-permute-start | bytes 3145736 | tf_op jit(solution)/shard_map/ppermute | solution.py:23
  3.9 0.0 copy-done.4
  3.9 0.1 copy.14.corners_ref
  4.0 12.2 %collective-permute-done.right_ref = f32[2,512,256]{2,1,0:T(8,128)S(1)} collective-permute-done((f32[2,512,256]{2,1,0:T(8,128)S(1)}, f32[2,512,256]{2,1,0:T(8,128)S(1)}, u32[]{:S(2)}, u32[]{:S(2)}) %collective-permute-start) | collective-permute-done | bytes 1048608 | tf_op jit(solution)/shard_map/ppermute | solution.py:23
  16.2 0.0 copy-done.1
  16.2 0.0 copy-done.2
  16.2 0.0 copy-done
  16.2 33.1 %patches.1 = (f32[2,512,512]{2,1,0:T(8,128)S(1)}, f32[2,512,256]{2,1,0:T(8,128)S(1)}, f32[2,8,128]{2,1,0:T(8,128)}) custom-call(s32[16,2]{1,0:T(8,128)S(1)} %copy.14.corners_ref, f32[2,512,512]{2,1,0:T(8,128)} %bitcast.11, f32[2,512,256]{2,1,0:T(8,128)S(1)} %collective-permute-done.right_ref, f32[2,8,128]{2,1,0:T(8,128)S(1)} %broadcast_in_dim.3.lower_ref, ...), custom_call_target="tpu_custom_call" | custom-call | flops 17179869184 | bytes 4194304 | tf_op jit(solution)/shard_map/patches/pallas_call | solution.py:195
  49.4 0.9 collective-permute-start.1
  50.2 13.5 %collective-permute-done.1 = f32[2,512,256]{2,1,0:T(8,128)S(1)} collective-permute-done((f32[2,512,256]{2,1,0:T(8,128)S(1)}, f32[2,512,256]{2,1,0:T(8,128)S(1)}, u32[]{:S(2)}, u32[]{:S(2)}) %collective-permute-start.1) | collective-permute-done | bytes 1048608 | tf_op jit(solution)/shard_map/ppermute | solution.py:23
  63.8 0.3 slice_add_fusion
  64.1 0.3 pad_maximum_fusion
  64.4 1.5 copy.15
  65.9 0.0 copy-start.3
  65.9 5.9 %all-to-all-start = ((f32[2,8,64,512]{3,2,0,1:T(8,128)}), f32[2,8,64,512]{3,2,0,1:T(8,128)S(1)}, u32[]{:S(2)}, u32[]{:S(2)}) async-start(f32[2,8,64,512]{3,2,0,1:T(8,128)} %copy.15), calls=%async_computation | async-start | bytes 4194304 | tf_op jit(solution)/shard_map/all_to_all | solution.py:332
  71.8 0.0 copy-done.3
  71.9 0.7 reshape.9.materials_ref
  72.5 46.0 %all-to-all-done = f32[2,8,64,512]{3,2,0,1:T(8,128)S(1)} async-done(((f32[2,8,64,512]{3,2,0,1:T(8,128)}), f32[2,8,64,512]{3,2,0,1:T(8,128)S(1)}, u32[]{:S(2)}, u32[]{:S(2)}) %all-to-all-start) | async-done | bytes 2097184 | tf_op jit(solution)/shard_map/all_to_all | solution.py:332
  118.5 1.6 copy.16.data_ref
  120.1 14.1 %fit.1 = f32[2,8,64,512]{3,2,1,0:T(8,128)} custom-call(f32[128]{0:T(128)} %reshape.9.materials_ref, f32[2,8,64,512]{3,2,1,0:T(8,128)} %copy.16.data_ref), custom_call_target="tpu_custom_call" | custom-call | tf_op jit(solution)/shard_map/fit/pallas_call | solution.py:297
  134.3 1.8 copy.17
  136.1 51.7 %all_to_all.10 = f32[2,8,64,512]{3,2,0,1:T(8,128)S(1)} all-to-all(f32[2,8,64,512]{3,2,0,1:T(8,128)S(1)} %copy.17), channel_id=1, replica_groups=mesh['energy'=8,'tile'=4] {'energy'}, dimensions={1} | all-to-all | bytes 4194304 | tf_op jit(solution)/shard_map/all_to_all | solution.py:334
  187.8 1.5 copy.18
  (1 shorter events, 0.0 us)
Async XLA Ops:
  0.0 16.2 %copy-start.1 = (bf16[256,256]{1,0:T(8,128)(2,1)S(1)}, bf16[256,256]{1,0:T(8,128)(2,1)}, u32[]{:S(2)}) copy-start(bf16[256,256]{1,0:T(8,128)(2,1)} %constant.12.cosine_ref) | copy-start | bytes 393220
  0.0 16.2 %copy-start.2 = (bf16[256,256]{1,0:T(8,128)(2,1)S(1)}, bf16[256,256]{1,0:T(8,128)(2,1)}, u32[]{:S(2)}) copy-start(bf16[256,256]{1,0:T(8,128)(2,1)} %constant.13.sine_ref) | copy-start | bytes 393220
  0.0 3.9 %copy-start.4 = (s32[1,16,2]{1,2,0:T(2,128)S(1)}, s32[1,16,2]{1,2,0:T(2,128)}, u32[]{:S(2)}) copy-start(s32[1,16,2]{1,2,0:T(2,128)} %param.10) | copy-start | bytes 388
  0.0 16.2 %copy-start = (f32[1,2,256,256]{3,2,1,0:T(8,128)S(1)}, f32[1,2,256,256]{3,2,1,0:T(8,128)}, u32[]{:S(2)}) copy-start(f32[1,2,256,256]{3,2,1,0:T(8,128)} %param.8) | copy-start | bytes 1572868
  1.4 14.8 %collective-permute-start = (f32[2,512,256]{2,1,0:T(8,128)S(1)}, f32[2,512,256]{2,1,0:T(8,128)S(1)}, u32[]{:S(2)}, u32[]{:S(2)}) collective-permute-start(f32[2,512,256]{2,1,0:T(8,128)S(1)} %slice.12), channel_id=1, source_target_pairs={{0,3},{1,0},{2,1},{3,2},{4,7},{5,4},{6,5},{7,6},{8,11},{9,8},{10,9... | collective-permute-start | bytes 3145736 | tf_op jit(solution)/shard_map/ppermute | solution.py:23
  49.4 14.4 %collective-permute-start.1 = (f32[2,512,256]{2,1,0:T(8,128)S(1)}, f32[2,512,256]{2,1,0:T(8,128)S(1)}, u32[]{:S(2)}, u32[]{:S(2)}) collective-permute-start(f32[2,512,256]{2,1,0:T(8,128)S(1)} %get-tuple-element.8), channel_id=1, source_target_pairs={{0,1},{1,2},{2,3},{3,0},{4,5},{5,6},{6,7},{7,4},{8,9},{9,10},{10,1... | collective-permute-start | bytes 3145736 | tf_op jit(solution)/shard_map/ppermute | solution.py:23
  65.9 5.9 %copy-start.3 = (f32[2,8,8]{2,1,0:T(8,128)S(1)}, f32[2,8,8]{2,1,0:T(8,128)}, u32[]{:S(2)}) copy-start(f32[2,8,8]{2,1,0:T(8,128)} %param.11) | copy-start | bytes 1540
  65.9 52.6 %all-to-all-start = ((f32[2,8,64,512]{3,2,0,1:T(8,128)}), f32[2,8,64,512]{3,2,0,1:T(8,128)S(1)}, u32[]{:S(2)}, u32[]{:S(2)}) async-start(f32[2,8,64,512]{3,2,0,1:T(8,128)} %copy.15), calls=%async_computation | async-start | bytes 4194304 | tf_op jit(solution)/shard_map/all_to_all | solution.py:332

commit v2 on v1

--- a/solution.py
+++ b/solution.py
@@ -244,26 +244,17 @@
     return gram, trace
 
 
-def fit_kernel(materials_ref, data_ref, out_ref, step_ref):
-    energies, rows, width = data_ref.shape[1:]
-    kinds = materials_ref.shape[0] // (2 * energies)
-    gram, trace = fit_scalars(materials_ref, energies, kinds)
-    rate = 1.0 / trace
-    for one in range(kinds):
-        for other in range(kinds):
-            unit = 1.0 if one == other else 0.0
-            step_ref[one * kinds + other] = unit - rate * gram[one][other]
-    tall, wide = 8, 256
-    across = width // wide
+def fit_columns(materials_ref, step_ref, data, spectra, energies, kinds, rate, begin, wide):
+    rows = data.shape[2]
+    tall = 16 if rows % 16 == 0 else 8
     pairs = [(part, energy) for part in range(2) for energy in range(energies)]
 
     def chunk(number, carry):
-        row = pl.multiple_of(number // across * tall, tall)
-        col = pl.multiple_of(number % across * wide, wide)
-        place = (pl.ds(row, tall), pl.ds(col, wide))
+        row = pl.multiple_of(number * tall, tall)
+        place = (pl.ds(row, tall), pl.ds(begin, wide))
         target = [None] * kinds
         for part, energy in pairs:
-            plane = data_ref[(part, energy) + place]
+            plane = data[(part, energy) + place]
             for kind in range(kinds):
                 term = materials_ref[(part * energies + energy) * kinds + kind] * plane
                 target[kind] = term if target[kind] is None else target[kind] + term
@@ -285,23 +276,176 @@
             for kind in range(kinds):
                 term = materials_ref[(part * energies + energy) * kinds + kind] * current[kind]
                 total = term if total is None else total + term
-            out_ref[(part, energy) + place] = total
+            spectra[(part, energy) + place] = total
         return carry
 
-    lax.fori_loop(0, rows // tall * across, chunk, 0)
-
-
-def fit_spectra(data, materials):
+    lax.fori_loop(0, rows // tall, chunk, 0)
+
+
+def exchange_kernel(
+    groups,
+    tiles,
+    materials_ref,
+    main_ref,
+    side_ref,
+    out_ref,
+    step_ref,
+    margin,
+    left,
+    data,
+    spectra,
+    margin_sems,
+    send_sems,
+    recv_sems,
+    own_sems,
+):
+    mesh_ids = pl.DeviceIdType.MESH
+    me = lax.axis_index("energy")
+    tile = lax.axis_index("tile")
+    after = lax.rem(tile + 1, tiles)
+    before = lax.rem(tile + tiles - 1, tiles)
+    tile_px = main_ref.shape[-1]
+    length = side_ref.shape[-1]
+    rows = tile_px // groups
+    kinds = materials_ref.shape[0] // (2 * groups)
+    offsets = sorted(range(1, groups), key=lambda offset: abs(offset - groups // 2))
+    peers = {offset: lax.rem(me + offset, groups) for offset in offsets}
+
+    barrier = pltpu.get_barrier_semaphore()
+    for neighbour in (after, before):
+        pl.semaphore_signal(barrier, inc=1, device_id=(me, neighbour), device_id_type=mesh_ids)
+    for offset in offsets:
+        pl.semaphore_signal(
+            barrier, inc=1, device_id=(peers[offset], tile), device_id_type=mesh_ids
+        )
+
+    gram, trace = fit_scalars(materials_ref, groups, kinds)
+    rate = 1.0 / trace
+    for one in range(kinds):
+        for other in range(kinds):
+            unit = 1.0 if one == other else 0.0
+            step_ref[one * kinds + other] = unit - rate * gram[one][other]
+    pl.semaphore_wait(barrier, groups + 1)
+
+    margin_copy = pltpu.make_async_remote_copy(
+        src_ref=side_ref,
+        dst_ref=margin,
+        send_sem=margin_sems.at[0],
+        recv_sem=margin_sems.at[1],
+        device_id=(me, after),
+        device_id_type=mesh_ids,
+    )
+    margin_copy.start()
+
+    def rows_of(group):
+        return pl.ds(pl.multiple_of(group * rows, rows), rows)
+
+    def outward(block):
+        columns = pl.ds(block * LANES, LANES)
+        source = left if block * LANES < length else main_ref
+        copies = [
+            pltpu.make_async_remote_copy(
+                src_ref=source.at[:, rows_of(peers[offset]), columns],
+                dst_ref=data.at[:, me, :, columns],
+                send_sem=send_sems.at[0, block, offset],
+                recv_sem=recv_sems.at[0, block, offset],
+                device_id=(peers[offset], tile),
+                device_id_type=mesh_ids,
+            )
+            for offset in offsets
+        ]
+        own = pltpu.make_async_copy(
+            source.at[:, rows_of(me), columns], data.at[:, me, :, columns], own_sems.at[0, block]
+        )
+        return copies, own
+
+    def homeward(block):
+        columns = pl.ds(block * LANES, LANES)
+        copies = [
+            pltpu.make_async_remote_copy(
+                src_ref=spectra.at[:, peers[offset], :, columns],
+                dst_ref=out_ref.at[:, rows_of(me), columns],
+                send_sem=send_sems.at[1, block, offset],
+                recv_sem=recv_sems.at[1, block, offset],
+                device_id=(peers[offset], tile),
+                device_id_type=mesh_ids,
+            )
+            for offset in offsets
+        ]
+        own = pltpu.make_async_copy(
+            spectra.at[:, me, :, columns], out_ref.at[:, rows_of(me), columns], own_sems.at[1, block]
+        )
+        return copies, own
+
+    def start(moves):
+        for copy in moves[0]:
+            copy.start()
+        moves[1].start()
+
+    blocks = tile_px // LANES
+    early = [block for block in range(blocks) if block * LANES >= length]
+    late = [block for block in range(blocks) if block * LANES < length]
+    going = {}
+    for block in early:
+        going[block] = outward(block)
+        start(going[block])
+    margin_copy.wait()
+    for block in late:
+        columns = slice(block * LANES, (block + 1) * LANES)
+        left[:, :, columns] = main_ref[:, :, columns] + margin[:, :, columns]
+    for block in late:
+        going[block] = outward(block)
+        start(going[block])
+    coming = {}
+    for block in early + late:
+        copies, own = going[block]
+        for copy in copies:
+            copy.wait_recv()
+        own.wait()
+        fit_columns(
+            materials_ref, step_ref, data, spectra, groups, kinds, rate, block * LANES, LANES
+        )
+        coming[block] = homeward(block)
+        start(coming[block])
+    for block in early + late:
+        for copy in going[block][0]:
+            copy.wait_send()
+        copies, own = coming[block]
+        own.wait()
+        for copy in copies:
+            copy.wait()
+
+
+def exchange_fit(main, side, materials):
+    groups = lax.axis_size("energy")
+    tiles = lax.axis_size("tile")
+    tile_px = main.shape[-1]
+    length = side.shape[-1]
     kinds = materials.shape[-1]
+    rows = tile_px // groups
+    blocks = tile_px // LANES
     vmem = pl.BlockSpec(memory_space=pltpu.VMEM)
     return pl.pallas_call(
-        fit_kernel,
-        out_shape=jax.ShapeDtypeStruct(data.shape, jnp.float32),
-        in_specs=[pl.BlockSpec(memory_space=pltpu.SMEM), vmem],
+        functools.partial(exchange_kernel, groups, tiles),
+        out_shape=jax.ShapeDtypeStruct(main.shape, jnp.float32),
+        in_specs=[pl.BlockSpec(memory_space=pltpu.SMEM), vmem, vmem],
         out_specs=vmem,
-        scratch_shapes=[pltpu.SMEM((kinds * kinds,), jnp.float32)],
-        name="fit",
-    )(materials.reshape(-1), data)
+        scratch_shapes=[
+            pltpu.SMEM((kinds * kinds,), jnp.float32),
+            pltpu.VMEM((2, tile_px, length), jnp.float32),
+            pltpu.VMEM((2, tile_px, length), jnp.float32),
+            pltpu.VMEM((2, groups, rows, tile_px), jnp.float32),
+            pltpu.VMEM((2, groups, rows, tile_px), jnp.float32),
+            pltpu.SemaphoreType.DMA((2,)),
+            pltpu.SemaphoreType.DMA((2, blocks, groups)),
+            pltpu.SemaphoreType.DMA((2, blocks, groups)),
+            pltpu.SemaphoreType.DMA((2, blocks)),
+        ],
+        compiler_params=pltpu.CompilerParams(
+            collective_id=0, has_side_effects=True, vmem_limit_bytes=32 * 1024 * 1024
+        ),
+        name="exchange",
+    )(materials.reshape(-1), main, side)
 
 
 def body(object_tiles, probe_wave, measured, positions, materials):
@@ -324,15 +468,8 @@
         from_above = shifted(below, "tile", row_step)
         main = main.at[:, :length, :].add(from_above[:, :, :tile_px])
         side = side.at[:, :length, :].add(from_above[:, :, tile_px:])
-    from_left = shifted(side, "tile", 1)
-    updated = jnp.concatenate([main[:, :, :length] + from_left, main[:, :, length:]], 2)
-    groups = lax.axis_size("energy")
-    group_rows = tile_px // groups
-    outgoing = updated.reshape(2, groups, group_rows, tile_px)
-    arrived = lax.all_to_all(outgoing, "energy", split_axis=1, concat_axis=1, tiled=True)
-    spectra = fit_spectra(arrived, materials)
-    returned = lax.all_to_all(spectra, "energy", split_axis=1, concat_axis=1, tiled=True)
-    return returned.reshape(1, 2, 1, tile_px, tile_px)
+    fitted = exchange_fit(main, side, materials)
+    return fitted.reshape(1, 2, 1, tile_px, tile_px)
 
 
 def solution(mesh):

time: 190 us -> 147 us (0.77)
  Pallas kernels: 47.3 us -> 129 us
  waiting for transfers between devices: 71.8 us -> 12.1 us
  blocking collectives: 51.7 us -> 0 us
  starting transfers between devices: 9.31 us -> 2.5 us
  local copies, waits for them, and re-layouts: 8.57 us -> 2.88 us
    pallas_call x1, Pallas kernels: 14.1 us -> 95.9 us  [exchange_fit(): pl.pallas_call(functools.partial(exchange_kernel, groups, tiles), out_sha...]
    all_to_all x1 -> x0, blocking collectives: 51.7 us -> none  [body(): lax.all_to_all(spectra, 'energy', split_axis=1, concat_axis=1, tiled=True)]
    all_to_all x1 -> x0, waiting for transfers between devices: 46 us -> none  [body(): lax.all_to_all(outgoing, 'energy', split_axis=1, concat_axis=1, tiled=True)]
    ppermute x2 -> x1, waiting for transfers between devices: 25.8 us -> 12.1 us  [shifted(): return lax.ppermute(value, axis, pairs)]
    all_to_all x1 -> x0, starting transfers between devices: 5.94 us -> none  [body(): lax.all_to_all(outgoing, 'energy', split_axis=1, concat_axis=1, tiled=True)]
    all_to_all x2 -> x0, local copies, waits for them, and re-layouts: 3.14 us -> none  [the longest x1 1.59 us: body(): lax.all_to_all(outgoing, 'energy', split_axis=1, concat_axis=1, tiled=True)]
    reshape x2 -> x1, local copies, waits for them, and re-layouts: 2.16 us -> 0.08 us  [exchange_fit(): materials.reshape(-1)]
  transfers between devices with their start and end apart: 3 -> 1, of which waited for: 3 -> 1; matrix products, arithmetic and copies ran while one was open for 0% -> 0% of each run, Pallas kernels for 0% -> 0%
where the time goes in v2:
time: 147 us
  Pallas kernels  129 us (88%)
  waiting for transfers between devices  12.1 us (8%)
  local copies, waits for them, and re-layouts  2.88 us (2%)
  starting transfers between devices  2.5 us (2%)
    pallas_call x1, Pallas kernels, exchange_fit(): pl.pallas_call(functools.partial(exchange_kernel, groups, tiles), out_sha...  95.9 us
    pallas_call x1, Pallas kernels, patch_update(): pl.pallas_call(functools.partial(patch_kernel, fold), out_shape=(jax.Shap...  33.3 us
    ppermute x1, waiting for transfers between devices, shifted(): return lax.ppermute(value, axis, pairs)  12.1 us
  transfers between devices with their start and end apart: 1, of which 1 were waited for; matrix products, arithmetic and copies ran while one was open for 0% of the time, Pallas kernels for 0%

profile of v2, /device:TPU:0, one launch (start us, length us, event | category | flops | bytes accessed | tf_op | source)
XLA Modules:
  0.0 146.8 jit_solution(7887328703823397553)
XLA Ops:
  0.0 0.0 copy-start.1
  0.0 0.0 copy-start.2
  0.0 0.0 copy-start.3
  0.0 0.0 copy-start.4
  0.0 0.0 copy-start
  0.0 1.4 slice.4
  1.4 2.5 %collective-permute-start = (f32[2,512,256]{2,1,0:T(8,128)S(1)}, f32[2,512,256]{2,1,0:T(8,128)S(1)}, u32[]{:S(2)}, u32[]{:S(2)}) collective-permute-start(f32[2,512,256]{2,1,0:T(8,128)S(1)} %slice.4), channel_id=1, source_target_pairs={{0,3},{1,0},{2,1},{3,2},{4,7},{5,4},{6,5},{7,6},{8,11},{9,8},{10,9... | collective-permute-start | bytes 3145736 | tf_op jit(solution)/shard_map/ppermute | solution.py:23
  3.9 0.0 copy-done.3
  3.9 0.1 reshape.6.materials_ref
  4.0 0.0 copy-done.4
  4.0 0.1 copy.8.corners_ref
  4.1 12.1 %collective-permute-done.right_ref = f32[2,512,256]{2,1,0:T(8,128)S(1)} collective-permute-done((f32[2,512,256]{2,1,0:T(8,128)S(1)}, f32[2,512,256]{2,1,0:T(8,128)S(1)}, u32[]{:S(2)}, u32[]{:S(2)}) %collective-permute-start) | collective-permute-done | bytes 1048608 | tf_op jit(solution)/shard_map/ppermute | solution.py:23
  16.2 0.0 copy-done.1
  16.2 0.0 copy-done.2
  16.2 0.0 copy-done
  16.2 33.3 %patches.1 = (f32[2,512,512]{2,1,0:T(8,128)S(1)}, f32[2,512,256]{2,1,0:T(8,128)S(1)}, f32[2,8,128]{2,1,0:T(8,128)}) custom-call(s32[16,2]{1,0:T(8,128)S(1)} %copy.8.corners_ref, f32[2,512,512]{2,1,0:T(8,128)} %bitcast.10, f32[2,512,256]{2,1,0:T(8,128)S(1)} %collective-permute-done.right_ref, f32[2,8,128]{2,1,0:T(8,128)S(1)} %broadcast_in_dim.3.lower_ref, ...), custom_call_target="tpu_custom_call" | custom-call | flops 17179869184 | bytes 4194304 | tf_op jit(solution)/shard_map/patches/pallas_call | solution.py:195
  49.5 95.9 %exchange.1 = f32[2,512,512]{2,1,0:T(8,128)S(1)} custom-call(f32[128]{0:T(128)S(1)} %reshape.6.materials_ref, f32[2,512,512]{2,1,0:T(8,128)S(1)} %get-tuple-element.7.main_ref, f32[2,512,256]{2,1,0:T(8,128)S(1)} %get-tuple-element.8.side_ref), custom_call_target="tpu_custom_call" | custom-call | tf_op jit(solution)/shard_map/exchange/pallas_call | solution.py:428
  145.4 1.3 copy.11
  (1 shorter events, 0.0 us)
Async XLA Ops:
  0.0 16.2 %copy-start.1 = (bf16[256,256]{1,0:T(8,128)(2,1)S(1)}, bf16[256,256]{1,0:T(8,128)(2,1)}, u32[]{:S(2)}) copy-start(bf16[256,256]{1,0:T(8,128)(2,1)} %constant.13.sine_ref) | copy-start | bytes 393220
  0.0 16.2 %copy-start.2 = (bf16[256,256]{1,0:T(8,128)(2,1)S(1)}, bf16[256,256]{1,0:T(8,128)(2,1)}, u32[]{:S(2)}) copy-start(bf16[256,256]{1,0:T(8,128)(2,1)} %constant.12.cosine_ref) | copy-start | bytes 393220
  0.0 3.9 %copy-start.3 = (f32[2,8,8]{2,1,0:T(8,128)S(1)}, f32[2,8,8]{2,1,0:T(8,128)}, u32[]{:S(2)}) copy-start(f32[2,8,8]{2,1,0:T(8,128)} %param.11) | copy-start | bytes 1540
  0.0 4.0 %copy-start.4 = (s32[1,16,2]{1,2,0:T(2,128)S(1)}, s32[1,16,2]{1,2,0:T(2,128)}, u32[]{:S(2)}) copy-start(s32[1,16,2]{1,2,0:T(2,128)} %param.10) | copy-start | bytes 388
  0.0 16.2 %copy-start = (f32[1,2,256,256]{3,2,1,0:T(8,128)S(1)}, f32[1,2,256,256]{3,2,1,0:T(8,128)}, u32[]{:S(2)}) copy-start(f32[1,2,256,256]{3,2,1,0:T(8,128)} %param.8) | copy-start | bytes 1572868
  1.4 14.8 %collective-permute-start = (f32[2,512,256]{2,1,0:T(8,128)S(1)}, f32[2,512,256]{2,1,0:T(8,128)S(1)}, u32[]{:S(2)}, u32[]{:S(2)}) collective-permute-start(f32[2,512,256]{2,1,0:T(8,128)S(1)} %slice.4), channel_id=1, source_target_pairs={{0,3},{1,0},{2,1},{3,2},{4,7},{5,4},{6,5},{7,6},{8,11},{9,8},{10,9... | collective-permute-start | bytes 3145736 | tf_op jit(solution)/shard_map/ppermute | solution.py:23

commit v3 on v2

--- a/solution.py
+++ b/solution.py
@@ -42,9 +42,8 @@
     )
 
 
-def transform(real_part, imag_part, left_ref, right_ref):
-    length = real_part.shape[0]
-    stacked = jnp.concatenate([real_part.astype(jnp.bfloat16), imag_part.astype(jnp.bfloat16)], 0)
+def transform(stacked, left_ref, right_ref):
+    length = stacked.shape[0] // 2
     inner = jnp.dot(left_ref[...], stacked, preferred_element_type=jnp.float32)
     inner = inner.astype(jnp.bfloat16)
     beside = jnp.concatenate([inner[:length], inner[length:]], 1)
@@ -76,39 +75,34 @@
         ref[place] = ref[place] + jnp.where(keep, one, other)
 
 
-def patch_kernel(
-    fold,
-    corners_ref,
-    object_ref,
-    right_ref,
-    lower_ref,
-    probe_ref,
-    measured_ref,
-    cosine_ref,
-    sine_ref,
-    main_out,
-    side_out,
-    below_out,
-    field,
-    gradient,
-    tables,
-    sems,
-):
+def patch_kernel(fold, inner, *refs):
+    corners_ref, object_ref, measured_ref, probe_ref, cosine_ref, sine_ref = refs[:6]
+    if inner:
+        (gradient,) = refs[6:7]
+        right_ref = lower_ref = None
+        rest = refs[7:]
+    else:
+        right_ref, lower_ref, begun_ref, main_out, side_out, below_out = refs[6:12]
+        gradient, *rest = refs[12:]
+    field, tables, wave, terms, order, sems = rest
     tile_px = object_ref.shape[-1]
     length = probe_ref.shape[-1]
     count = measured_ref.shape[0]
     blocks = tile_px // LANES
+    width = blocks + length // LANES
     top = pl.ds(0, tile_px)
     bottom = pl.ds(tile_px, length)
     moves = []
-    for block in range(blocks + length // LANES):
+    for block in range(blocks if inner else width):
         ref, at = (object_ref, block) if block < blocks else (right_ref, block - blocks)
         columns = pl.ds(at * LANES, LANES)
         moves.append((ref.at[:, :, columns], field.at[:, block, top, :]))
         if fold:
             source = ref.at[:, pl.ds(0, length), columns]
+        elif not inner:
+            source = lower_ref.at[:, :, pl.ds(block * LANES, LANES)]
         else:
-            source = lower_ref.at[:, :, pl.ds(block * LANES, LANES)]
+            continue
         moves.append((source, field.at[:, block, bottom, :]))
     copies = [
         pltpu.make_async_copy(source, target, sems.at[number])
@@ -120,39 +114,74 @@
     sine = sine_ref[...]
     tables[0] = joined(cosine, sine, -sine, cosine)
     tables[1] = joined(cosine, -sine, sine, cosine)
-    gradient[...] = jnp.zeros_like(gradient)
+    if inner:
+        gradient[...] = jnp.zeros_like(gradient)
+    else:
+        gradient[...] = begun_ref[...]
+    terms[...] = jnp.zeros_like(terms)
+
+    limit = tile_px - length
+
+    def choose(number, found):
+        order[found] = number
+        within = corners_ref[number, 1] <= limit
+        if not fold:
+            within = jnp.logical_and(within, corners_ref[number, 0] <= limit)
+        return found + jnp.where(within, int(inner), 1 - int(inner))
+
+    total = lax.fori_loop(0, count, choose, 0)
     for copy in copies:
         copy.wait()
 
-    def step(number, carry):
+    def corner(turn):
+        number = order[turn]
         row = corners_ref[number, 0]
         col = corners_ref[number, 1]
         block = col // LANES
-        shift = col - block * LANES
+        return number, row, block, col - block * LANES
+
+    def gather(turn):
+        _, row, block, shift = corner(turn)
         piece_real = window(field, 0, row, block, shift, length)
         piece_imag = window(field, 1, row, block, shift, length)
         probe_real = probe_ref[0]
         probe_imag = probe_ref[1]
         exit_real = probe_real * piece_real - probe_imag * piece_imag
         exit_imag = probe_real * piece_imag + probe_imag * piece_real
-        far_real, far_imag = transform(exit_real, exit_imag, tables.at[0], tables.at[1])
+        wave[:length, :] = exit_real.astype(jnp.bfloat16)
+        wave[length:, :] = exit_imag.astype(jnp.bfloat16)
+
+    def scatter(turn):
+        _, row, block, shift = corner(turn)
+        add_window(gradient, 0, row, block, shift, terms[0])
+        add_window(gradient, 1, row, block, shift, terms[1])
+
+    def step(turn, carry):
+        stacked = wave[...]
+        scatter(jnp.maximum(turn - 1, 0))
+        far_real, far_imag = transform(stacked, tables.at[0], tables.at[1])
+        gather(jnp.minimum(turn + 1, total - 1))
         square = far_real * far_real + far_imag * far_imag
         scale = lax.rsqrt(jnp.maximum(square, amplitude_floor * amplitude_floor))
-        factor = measured_ref[number].astype(jnp.float32) * scale - 1.0
-        back_real, back_imag = transform(
-            factor * far_real, factor * far_imag, tables.at[1], tables.at[0]
+        factor = measured_ref[order[turn]].astype(jnp.float32) * scale - 1.0
+        change = jnp.concatenate(
+            [(factor * far_real).astype(jnp.bfloat16), (factor * far_imag).astype(jnp.bfloat16)], 0
         )
+        back_real, back_imag = transform(change, tables.at[1], tables.at[0])
         probe_real = probe_ref[0]
         probe_imag = probe_ref[1]
-        add_window(
-            gradient, 0, row, block, shift, probe_real * back_real + probe_imag * back_imag
-        )
-        add_window(
-            gradient, 1, row, block, shift, probe_real * back_imag - probe_imag * back_real
-        )
+        terms[0] = probe_real * back_real + probe_imag * back_imag
+        terms[1] = probe_real * back_imag - probe_imag * back_real
         return carry
 
-    lax.fori_loop(0, count, step, 0)
+    @pl.when(total > 0)
+    def _():
+        gather(0)
+        lax.fori_loop(0, total, step, 0)
+        scatter(total - 1)
+
+    if inner:
+        return
     peak = jnp.max(probe_ref[0] * probe_ref[0] + probe_ref[1] * probe_ref[1])
     rows = 64
 
@@ -160,11 +189,11 @@
         place = (pl.ds(pl.multiple_of(number * rows, rows), rows), slice(None))
         beyond = pl.ds(pl.multiple_of(tile_px + number * rows, rows), rows)
         for part in range(2):
-            for block in range(blocks + length // LANES):
-                total = gradient[(part, block) + place]
+            for block in range(width):
+                value = gradient[(part, block) + place]
                 if wrapped:
-                    total = total + gradient[part, block, beyond, :]
-                share = total / peak
+                    value = value + gradient[part, block, beyond, :]
+                share = value / peak
                 if block < blocks:
                     columns = slice(block * LANES, (block + 1) * LANES)
                     main_out[part, place[0], columns] = field[(part, block) + place] + share
@@ -178,50 +207,49 @@
     if fold:
         below_out[...] = jnp.zeros_like(below_out)
     else:
-        for block in range(blocks + length // LANES):
+        for block in range(width):
             columns = slice(block * LANES, (block + 1) * LANES)
             below_out[:, :, columns] = gradient[:, block, tile_px:, :] / peak
 
 
-def patch_update(own_object, right_strip, lower_strip, probe, measured, corners, fold):
+def patch_call(own_object, probe, measured, corners, fold, margins=()):
     tile_px = own_object.shape[-1]
     length = probe.shape[-1]
     count = measured.shape[0]
     width = tile_px + length
     cosine, sine = fourier_parts(length)
+    inner = not margins
     below = (2, 8, LANES) if fold else (2, length, width)
     vmem = pl.BlockSpec(memory_space=pltpu.VMEM)
     anywhere = pl.BlockSpec(memory_space=pl.ANY)
+    sums = (2, width // LANES, width, LANES)
+    if inner:
+        shapes = [sums]
+    else:
+        shapes = [(2, tile_px, tile_px), (2, tile_px, length), below]
+    scratch = [
+        pltpu.VMEM(sums, jnp.float32),
+        pltpu.VMEM((2, 2 * length, 2 * length), jnp.bfloat16),
+        pltpu.VMEM((2 * length, length), jnp.bfloat16),
+        pltpu.VMEM((2, length, length), jnp.float32),
+        pltpu.SMEM((count + 1,), jnp.int32),
+        pltpu.SemaphoreType.DMA((2 * (width // LANES),)),
+    ]
+    if not inner:
+        scratch = [pltpu.VMEM(sums, jnp.float32)] + scratch
     return pl.pallas_call(
-        functools.partial(patch_kernel, fold),
-        out_shape=(
-            jax.ShapeDtypeStruct((2, tile_px, tile_px), jnp.float32),
-            jax.ShapeDtypeStruct((2, tile_px, length), jnp.float32),
-            jax.ShapeDtypeStruct(below, jnp.float32),
+        functools.partial(patch_kernel, fold, inner),
+        out_shape=[jax.ShapeDtypeStruct(shape, jnp.float32) for shape in shapes],
+        in_specs=[pl.BlockSpec(memory_space=pltpu.SMEM), anywhere, vmem, vmem, vmem, vmem]
+        + ([] if inner else [anywhere, anywhere, vmem]),
+        out_specs=[vmem] * len(shapes),
+        scratch_shapes=scratch,
+        compiler_params=pltpu.CompilerParams(vmem_limit_bytes=40 * 1024 * 1024),
+        cost_estimate=pl.CostEstimate(
+            flops=32 * count * length**3, bytes_accessed=16 * tile_px * tile_px, transcendentals=0
         ),
-        in_specs=[
-            pl.BlockSpec(memory_space=pltpu.SMEM),
-            anywhere,
-            anywhere,
-            anywhere,
-            vmem,
-            vmem,
-            vmem,
-            vmem,
-        ],
-        out_specs=(vmem, vmem, vmem),
-        scratch_shapes=[
-            pltpu.VMEM((2, width // LANES, width, LANES), jnp.float32),
-            pltpu.VMEM((2, width // LANES, width, LANES), jnp.float32),
-            pltpu.VMEM((2, 2 * length, 2 * length), jnp.bfloat16),
-            pltpu.SemaphoreType.DMA((2 * (width // LANES),)),
-        ],
-        compiler_params=pltpu.CompilerParams(vmem_limit_bytes=48 * 1024 * 1024),
-        cost_estimate=pl.CostEstimate(
-            flops=64 * count * length**3, bytes_accessed=16 * tile_px * tile_px, transcendentals=0
-        ),
-        name="patches",
-    )(corners, own_object, right_strip, lower_strip, probe, measured, cosine, sine)
+        name="patches_inner" if inner else "patches_outer",
+    )(corners, own_object, measured, probe, cosine, sine, *margins)
 
 
 def fit_scalars(materials_ref, energies, kinds):
@@ -461,9 +489,9 @@
     else:
         widened = jnp.concatenate([own_object[:, :length], right_strip[:, :length]], 2)
         lower_strip = shifted(widened, "tile", -row_step)
-    main, side, below = patch_update(
-        own_object, right_strip, lower_strip, probe_wave[0], measured[0, 0], positions[0], fold
-    )
+    shared = (own_object, probe_wave[0], measured[0, 0], positions[0], fold)
+    (begun,) = patch_call(*shared)
+    main, side, below = patch_call(*shared, margins=(right_strip, lower_strip, begun))
     if not fold:
         from_above = shifted(below, "tile", row_step)
         main = main.at[:, :length, :].add(from_above[:, :, :tile_px])

time: 147 us -> 135 us (0.918)
  waiting for transfers between devices: 12.1 us -> 0.01 us
  local copies, waits for them, and re-layouts: 2.88 us -> 8.35 us
  Pallas kernels: 129 us -> 124 us
    ppermute x1, waiting for transfers between devices: 12.1 us -> 0.01 us  [shifted(): return lax.ppermute(value, axis, pairs)]
    pallas_call x1 -> x2, Pallas kernels: 33.3 us -> 28.7 us  [patch_call(): pl.pallas_call(functools.partial(patch_kernel, fold, inner), out_shape=[j...]
    unnamed x11 -> x15, local copies, waits for them, and re-layouts: 1.34 us -> 5.77 us
  transfers between devices with their start and end apart: 1 -> 1, of which waited for: 1 -> 0; matrix products, arithmetic and copies ran while one was open for 0% -> 0% of each run, Pallas kernels for 0% -> 9%
where the time goes in v3:
time: 135 us
  Pallas kernels  124 us (92%)
  local copies, waits for them, and re-layouts  8.35 us (6%)
  starting transfers between devices  2.44 us (2%)
    pallas_call x1, Pallas kernels, exchange_fit(): pl.pallas_call(functools.partial(exchange_kernel, groups, tiles), out_sha...  95.1 us
    pallas_call x2, Pallas kernels, patch_call(): pl.pallas_call(functools.partial(patch_kernel, fold, inner), out_shape=[j...  28.7 us
    unnamed x15, local copies, waits for them, and re-layouts  5.77 us
  transfers between devices with their start and end apart: 1, of which 0 were waited for; matrix products, arithmetic and copies ran while one was open for 0% of the time, Pallas kernels for 9%

profile of v3, /device:TPU:0, one launch (start us, length us, event | category | flops | bytes accessed | tf_op | source)
XLA Modules:
  0.0 134.6 jit_solution(13788520454992879951)
XLA Ops:
  0.0 0.0 copy-start
  0.0 0.0 copy-start.6
  0.0 0.0 copy-start.5
  0.0 2.4 %slice.4 = f32[2,512,256]{2,1,0:T(8,128)} slice(f32[2,512,512]{2,1,0:T(8,128)} %bitcast.8), slice={[0:2], [0:512], [0:256]} | slice | bytes 2097152 | tf_op jit(solution)/shard_map/slice | solution.py:486
  2.4 2.4 %collective-permute-start = (f32[2,512,256]{2,1,0:T(8,128)}, f32[2,512,256]{2,1,0:T(8,128)S(1)}, u32[]{:S(2)}, u32[]{:S(2)}) collective-permute-start(f32[2,512,256]{2,1,0:T(8,128)} %slice.4), channel_id=1, source_target_pairs={{0,3},{1,0},{2,1},{3,2},{4,7},{5,4},{6,5},{7,6},{8,11},{9,8},{10,9... | collective-permute-start | bytes 3145736 | tf_op jit(solution)/shard_map/ppermute | solution.py:23
  4.9 0.0 copy-done.6
  4.9 0.1 copy.11.refs_0_
  4.9 0.0 copy-done.5
  4.9 0.1 reshape.6.materials_ref
  5.0 0.0 copy-done
  5.0 0.0 copy-start.1
  5.1 1.6 %copy-done.1 = bf16[1,1,16,256,256]{4,3,2,1,0:T(8,128)(2,1)S(1)} copy-done((bf16[1,1,16,256,256]{4,3,2,1,0:T(8,128)(2,1)S(1)}, bf16[1,1,16,256,256]{4,3,2,1,0:T(8,128)(2,1)}, u32[]{:S(2)}) %copy-start.1) | copy-done | bytes 2097176
  6.6 0.0 copy-start.2
  6.6 1.0 copy-done.2
  7.7 0.0 copy-start.3
  7.7 0.9 copy-done.3
  8.6 0.0 copy-start.4
  8.6 0.9 copy-done.4
  9.5 12.3 %patches_inner.1.refs_8_ = f32[2,6,768,128]{3,2,1,0:T(8,128)S(1)} custom-call(s32[16,2]{1,0:T(8,128)S(1)} %copy.11.refs_0_, f32[2,512,512]{2,1,0:T(8,128)S(1)} %bitcast.9, bf16[16,256,256]{2,1,0:T(8,128)(2,1)S(1)} %bitcast.11, f32[2,256,256]{2,1,0:T(8,128)S(1)} %bitcast.13, bf16[256,256]{1,0:T(8,128)(2,1)S(1)} %copy-done.3, bf16[256,256]{1,0:T(8,128)(2,1)S(1)} %copy-done.4), custom_call_target="tpu_custom_call" | custom-call | flops 8589934592 | bytes 4194304 | tf_op jit(solution)/shard_map/patches_inner/pallas_call | solution.py:240
  21.8 0.0 collective-permute-done.refs_6_
  21.8 16.4 %patches_outer.1 = (f32[2,512,512]{2,1,0:T(8,128)S(1)}, f32[2,512,256]{2,1,0:T(8,128)S(1)}, f32[2,8,128]{2,1,0:T(8,128)}) custom-call(s32[16,2]{1,0:T(8,128)S(1)} %copy.11.refs_0_, f32[2,512,512]{2,1,0:T(8,128)S(1)} %bitcast.10, bf16[16,256,256]{2,1,0:T(8,128)(2,1)S(1)} %bitcast.12, f32[2,256,256]{2,1,0:T(8,128)S(1)} %bitcast.14, ...), custom_call_target="tpu_custom_call" | custom-call | flops 8589934592 | bytes 4194304 | tf_op jit(solution)/shard_map/patches_outer/pallas_call | solution.py:240
  38.2 95.1 %exchange.1 = f32[2,512,512]{2,1,0:T(8,128)S(1)} custom-call(f32[128]{0:T(128)S(1)} %reshape.6.materials_ref, f32[2,512,512]{2,1,0:T(8,128)S(1)} %get-tuple-element.7.main_ref, f32[2,512,256]{2,1,0:T(8,128)S(1)} %get-tuple-element.8.side_ref), custom_call_target="tpu_custom_call" | custom-call | tf_op jit(solution)/shard_map/exchange/pallas_call | solution.py:456
  133.3 1.3 copy.14
  (1 shorter events, 0.0 us)
Async XLA Ops:
  0.0 5.0 %copy-start = (f32[1,2,1,512,512]{4,3,2,1,0:T(8,128)S(1)}, f32[1,2,1,512,512]{4,3,2,1,0:T(8,128)}, u32[]{:S(2)}) copy-start(f32[1,2,1,512,512]{4,3,2,1,0:T(8,128)} %param.9) | copy-start | bytes 6291460
  0.0 4.9 %copy-start.6 = (s32[1,16,2]{1,2,0:T(2,128)S(1)}, s32[1,16,2]{1,2,0:T(2,128)}, u32[]{:S(2)}) copy-start(s32[1,16,2]{1,2,0:T(2,128)} %param.12) | copy-start | bytes 388
  0.0 4.9 %copy-start.5 = (f32[2,8,8]{2,1,0:T(8,128)S(1)}, f32[2,8,8]{2,1,0:T(8,128)}, u32[]{:S(2)}) copy-start(f32[2,8,8]{2,1,0:T(8,128)} %param.13) | copy-start | bytes 1540
  2.4 19.4 %collective-permute-start = (f32[2,512,256]{2,1,0:T(8,128)}, f32[2,512,256]{2,1,0:T(8,128)S(1)}, u32[]{:S(2)}, u32[]{:S(2)}) collective-permute-start(f32[2,512,256]{2,1,0:T(8,128)} %slice.4), channel_id=1, source_target_pairs={{0,3},{1,0},{2,1},{3,2},{4,7},{5,4},{6,5},{7,6},{8,11},{9,8},{10,9... | collective-permute-start | bytes 3145736 | tf_op jit(solution)/shard_map/ppermute | solution.py:23
  5.0 1.6 %copy-start.1 = (bf16[1,1,16,256,256]{4,3,2,1,0:T(8,128)(2,1)S(1)}, bf16[1,1,16,256,256]{4,3,2,1,0:T(8,128)(2,1)}, u32[]{:S(2)}) copy-start(bf16[1,1,16,256,256]{4,3,2,1,0:T(8,128)(2,1)} %param.11) | copy-start | bytes 6291460
  6.6 1.0 copy-start.2
  7.7 0.9 copy-start.3
  8.6 0.9 copy-start.4

commit v4 on v3

--- a/solution.py
+++ b/solution.py
@@ -84,7 +84,7 @@
     else:
         right_ref, lower_ref, begun_ref, main_out, side_out, below_out = refs[6:12]
         gradient, *rest = refs[12:]
-    field, tables, wave, terms, order, sems = rest
+    field, tables, wave, change, terms, order, sems = rest
     tile_px = object_ref.shape[-1]
     length = probe_ref.shape[-1]
     count = measured_ref.shape[0]
@@ -156,28 +156,46 @@
         add_window(gradient, 0, row, block, shift, terms[0])
         add_window(gradient, 1, row, block, shift, terms[1])
 
-    def step(turn, carry):
-        stacked = wave[...]
-        scatter(jnp.maximum(turn - 1, 0))
-        far_real, far_imag = transform(stacked, tables.at[0], tables.at[1])
-        gather(jnp.minimum(turn + 1, total - 1))
+    def outward(turn):
+        far_real, far_imag = transform(wave[...], tables.at[0], tables.at[1])
         square = far_real * far_real + far_imag * far_imag
         scale = lax.rsqrt(jnp.maximum(square, amplitude_floor * amplitude_floor))
         factor = measured_ref[order[turn]].astype(jnp.float32) * scale - 1.0
-        change = jnp.concatenate(
-            [(factor * far_real).astype(jnp.bfloat16), (factor * far_imag).astype(jnp.bfloat16)], 0
-        )
-        back_real, back_imag = transform(change, tables.at[1], tables.at[0])
+        return (factor * far_real).astype(jnp.bfloat16), (factor * far_imag).astype(jnp.bfloat16)
+
+    def keep(parts):
+        change[:length, :] = parts[0]
+        change[length:, :] = parts[1]
+
+    def homeward():
+        back_real, back_imag = transform(change[...], tables.at[1], tables.at[0])
         probe_real = probe_ref[0]
         probe_imag = probe_ref[1]
-        terms[0] = probe_real * back_real + probe_imag * back_imag
-        terms[1] = probe_real * back_imag - probe_imag * back_real
+        return (
+            probe_real * back_real + probe_imag * back_imag,
+            probe_real * back_imag - probe_imag * back_real,
+        )
+
+    def step(turn, carry):
+        scatter(jnp.maximum(turn - 1, 0))
+        parts = outward(turn + 1)
+        back = homeward()
+        keep(parts)
+        gather(jnp.minimum(turn + 2, total - 1))
+        terms[0] = back[0]
+        terms[1] = back[1]
         return carry
 
     @pl.when(total > 0)
     def _():
         gather(0)
-        lax.fori_loop(0, total, step, 0)
+        keep(outward(0))
+        gather(jnp.minimum(1, total - 1))
+        lax.fori_loop(0, total - 1, step, 0)
+        scatter(jnp.maximum(total - 2, 0))
+        back = homeward()
+        terms[0] = back[0]
+        terms[1] = back[1]
         scatter(total - 1)
 
     if inner:
@@ -230,6 +248,7 @@
     scratch = [
         pltpu.VMEM(sums, jnp.float32),
         pltpu.VMEM((2, 2 * length, 2 * length), jnp.bfloat16),
+        pltpu.VMEM((2 * length, length), jnp.bfloat16),
         pltpu.VMEM((2 * length, length), jnp.bfloat16),
         pltpu.VMEM((2, length, length), jnp.float32),
         pltpu.SMEM((count + 1,), jnp.int32),
@@ -347,12 +366,6 @@
             barrier, inc=1, device_id=(peers[offset], tile), device_id_type=mesh_ids
         )
 
-    gram, trace = fit_scalars(materials_ref, groups, kinds)
-    rate = 1.0 / trace
-    for one in range(kinds):
-        for other in range(kinds):
-            unit = 1.0 if one == other else 0.0
-            step_ref[one * kinds + other] = unit - rate * gram[one][other]
     pl.semaphore_wait(barrier, groups + 1)
 
     margin_copy = pltpu.make_async_remote_copy(
@@ -417,6 +430,13 @@
     for block in early:
         going[block] = outward(block)
         start(going[block])
+
+    gram, trace = fit_scalars(materials_ref, groups, kinds)
+    rate = 1.0 / trace
+    for one in range(kinds):
+        for other in range(kinds):
+            unit = 1.0 if one == other else 0.0
+            step_ref[one * kinds + other] = unit - rate * gram[one][other]
     margin_copy.wait()
     for block in late:
         columns = slice(block * LANES, (block + 1) * LANES)

time: 135 us -> 130 us (0.963)
  Pallas kernels: 124 us -> 119 us
    pallas_call x2, Pallas kernels: 28.7 us -> 23.6 us  [patch_call(): pl.pallas_call(functools.partial(patch_kernel, fold, inner), out_shape=[j...]
  transfers between devices with their start and end apart: 1 -> 1, of which waited for: 0 -> 0; matrix products, arithmetic and copies ran while one was open for 0% -> 0% of each run, Pallas kernels for 9% -> 8%
where the time goes in v4:
time: 130 us
  Pallas kernels  119 us (92%)
  local copies, waits for them, and re-layouts  8.35 us (6%)
  starting transfers between devices  2.44 us (2%)
    pallas_call x1, Pallas kernels, exchange_fit(): pl.pallas_call(functools.partial(exchange_kernel, groups, tiles), out_sha...  95.1 us
    pallas_call x2, Pallas kernels, patch_call(): pl.pallas_call(functools.partial(patch_kernel, fold, inner), out_shape=[j...  23.6 us
    unnamed x15, local copies, waits for them, and re-layouts  5.77 us
  transfers between devices with their start and end apart: 1, of which 0 were waited for; matrix products, arithmetic and copies ran while one was open for 0% of the time, Pallas kernels for 8%

profile of v4, /device:TPU:0, one launch (start us, length us, event | category | flops | bytes accessed | tf_op | source)
XLA Modules:
  0.0 129.6 jit_solution(15918706771643523378)
XLA Ops:
  0.0 0.0 copy-start
  0.0 0.0 copy-start.6
  0.0 0.0 copy-start.5
  0.0 2.4 %slice.4 = f32[2,512,256]{2,1,0:T(8,128)} slice(f32[2,512,512]{2,1,0:T(8,128)} %bitcast.8), slice={[0:2], [0:512], [0:256]} | slice | bytes 2097152 | tf_op jit(solution)/shard_map/slice | solution.py:506
  2.4 2.4 %collective-permute-start = (f32[2,512,256]{2,1,0:T(8,128)}, f32[2,512,256]{2,1,0:T(8,128)S(1)}, u32[]{:S(2)}, u32[]{:S(2)}) collective-permute-start(f32[2,512,256]{2,1,0:T(8,128)} %slice.4), channel_id=1, source_target_pairs={{0,3},{1,0},{2,1},{3,2},{4,7},{5,4},{6,5},{7,6},{8,11},{9,8},{10,9... | collective-permute-start | bytes 3145736 | tf_op jit(solution)/shard_map/ppermute | solution.py:23
  4.9 0.0 copy-done.6
  4.9 0.1 copy.11.refs_0_
  4.9 0.0 copy-done.5
  4.9 0.1 reshape.6.materials_ref
  5.0 0.0 copy-done
  5.0 0.0 copy-start.1
  5.1 1.6 %copy-done.1 = bf16[1,1,16,256,256]{4,3,2,1,0:T(8,128)(2,1)S(1)} copy-done((bf16[1,1,16,256,256]{4,3,2,1,0:T(8,128)(2,1)S(1)}, bf16[1,1,16,256,256]{4,3,2,1,0:T(8,128)(2,1)}, u32[]{:S(2)}) %copy-start.1) | copy-done | bytes 2097176
  6.6 0.0 copy-start.2
  6.6 1.0 copy-done.2
  7.7 0.0 copy-start.3
  7.7 0.9 copy-done.3
  8.6 0.0 copy-start.4
  8.6 0.9 copy-done.4
  9.5 10.1 %patches_inner.1.refs_8_ = f32[2,6,768,128]{3,2,1,0:T(8,128)S(1)} custom-call(s32[16,2]{1,0:T(8,128)S(1)} %copy.11.refs_0_, f32[2,512,512]{2,1,0:T(8,128)S(1)} %bitcast.9, bf16[16,256,256]{2,1,0:T(8,128)(2,1)S(1)} %bitcast.11, f32[2,256,256]{2,1,0:T(8,128)S(1)} %bitcast.13, bf16[256,256]{1,0:T(8,128)(2,1)S(1)} %copy-done.3, bf16[256,256]{1,0:T(8,128)(2,1)S(1)} %copy-done.4), custom_call_target="tpu_custom_call" | custom-call | flops 8589934592 | bytes 4194304 | tf_op jit(solution)/shard_map/patches_inner/pallas_call | solution.py:259
  19.6 0.0 collective-permute-done.refs_6_
  19.6 13.5 %patches_outer.1 = (f32[2,512,512]{2,1,0:T(8,128)S(1)}, f32[2,512,256]{2,1,0:T(8,128)S(1)}, f32[2,8,128]{2,1,0:T(8,128)}) custom-call(s32[16,2]{1,0:T(8,128)S(1)} %copy.11.refs_0_, f32[2,512,512]{2,1,0:T(8,128)S(1)} %bitcast.10, bf16[16,256,256]{2,1,0:T(8,128)(2,1)S(1)} %bitcast.12, f32[2,256,256]{2,1,0:T(8,128)S(1)} %bitcast.14, ...), custom_call_target="tpu_custom_call" | custom-call | flops 8589934592 | bytes 4194304 | tf_op jit(solution)/shard_map/patches_outer/pallas_call | solution.py:259
  33.1 95.1 %exchange.1 = f32[2,512,512]{2,1,0:T(8,128)S(1)} custom-call(f32[128]{0:T(128)S(1)} %reshape.6.materials_ref, f32[2,512,512]{2,1,0:T(8,128)S(1)} %get-tuple-element.7.main_ref, f32[2,512,256]{2,1,0:T(8,128)S(1)} %get-tuple-element.8.side_ref), custom_call_target="tpu_custom_call" | custom-call | tf_op jit(solution)/shard_map/exchange/pallas_call | solution.py:476
  128.3 1.3 %copy.14 = f32[1,2,1,512,512]{4,3,2,1,0:T(8,128)} copy(f32[1,2,1,512,512]{4,3,2,1,0:T(8,128)S(1)} %bitcast.7) | data formatting | bytes 4194304
  (1 shorter events, 0.0 us)
Async XLA Ops:
  0.0 5.0 %copy-start = (f32[1,2,1,512,512]{4,3,2,1,0:T(8,128)S(1)}, f32[1,2,1,512,512]{4,3,2,1,0:T(8,128)}, u32[]{:S(2)}) copy-start(f32[1,2,1,512,512]{4,3,2,1,0:T(8,128)} %param.9) | copy-start | bytes 6291460
  0.0 4.9 %copy-start.6 = (s32[1,16,2]{1,2,0:T(2,128)S(1)}, s32[1,16,2]{1,2,0:T(2,128)}, u32[]{:S(2)}) copy-start(s32[1,16,2]{1,2,0:T(2,128)} %param.12) | copy-start | bytes 388
  0.0 4.9 %copy-start.5 = (f32[2,8,8]{2,1,0:T(8,128)S(1)}, f32[2,8,8]{2,1,0:T(8,128)}, u32[]{:S(2)}) copy-start(f32[2,8,8]{2,1,0:T(8,128)} %param.13) | copy-start | bytes 1540
  2.4 17.2 %collective-permute-start = (f32[2,512,256]{2,1,0:T(8,128)}, f32[2,512,256]{2,1,0:T(8,128)S(1)}, u32[]{:S(2)}, u32[]{:S(2)}) collective-permute-start(f32[2,512,256]{2,1,0:T(8,128)} %slice.4), channel_id=1, source_target_pairs={{0,3},{1,0},{2,1},{3,2},{4,7},{5,4},{6,5},{7,6},{8,11},{9,8},{10,9... | collective-permute-start | bytes 3145736 | tf_op jit(solution)/shard_map/ppermute | solution.py:23
  5.0 1.6 %copy-start.1 = (bf16[1,1,16,256,256]{4,3,2,1,0:T(8,128)(2,1)S(1)}, bf16[1,1,16,256,256]{4,3,2,1,0:T(8,128)(2,1)}, u32[]{:S(2)}) copy-start(bf16[1,1,16,256,256]{4,3,2,1,0:T(8,128)(2,1)} %param.11) | copy-start | bytes 6291460
  6.6 1.0 copy-start.2
  7.7 0.9 copy-start.3
  8.6 0.9 copy-start.4

commit v5 on v4

--- a/solution.py
+++ b/solution.py
@@ -26,9 +26,8 @@
 def fourier_parts(length):
     counter = np.arange(length, dtype=np.int64)
     angles = 2.0 * math.pi / length * (counter[:, None] * counter[None, :] % length)
-    return (
-        jnp.asarray(np.cos(angles), jnp.float32).astype(jnp.bfloat16),
-        jnp.asarray(np.sin(angles), jnp.float32).astype(jnp.bfloat16),
+    return jnp.asarray(
+        np.stack([np.cos(angles), np.sin(angles)]).astype(np.float32).astype(jnp.bfloat16)
     )
 
 
@@ -76,14 +75,14 @@
 
 
 def patch_kernel(fold, inner, *refs):
-    corners_ref, object_ref, measured_ref, probe_ref, cosine_ref, sine_ref = refs[:6]
+    corners_ref, object_ref, measured_ref, probe_ref, fourier_ref = refs[:5]
     if inner:
-        (gradient,) = refs[6:7]
+        (gradient,) = refs[5:6]
         right_ref = lower_ref = None
-        rest = refs[7:]
+        rest = refs[6:]
     else:
-        right_ref, lower_ref, begun_ref, main_out, side_out, below_out = refs[6:12]
-        gradient, *rest = refs[12:]
+        right_ref, lower_ref, begun_ref, main_out, side_out, below_out = refs[5:11]
+        gradient, *rest = refs[11:]
     field, tables, wave, change, terms, order, sems = rest
     tile_px = object_ref.shape[-1]
     length = probe_ref.shape[-1]
@@ -110,8 +109,8 @@
     ]
     for copy in copies:
         copy.start()
-    cosine = cosine_ref[...]
-    sine = sine_ref[...]
+    cosine = fourier_ref[0]
+    sine = fourier_ref[1]
     tables[0] = joined(cosine, sine, -sine, cosine)
     tables[1] = joined(cosine, -sine, sine, cosine)
     if inner:
@@ -235,7 +234,6 @@
     length = probe.shape[-1]
     count = measured.shape[0]
     width = tile_px + length
-    cosine, sine = fourier_parts(length)
     inner = not margins
     below = (2, 8, LANES) if fold else (2, length, width)
     vmem = pl.BlockSpec(memory_space=pltpu.VMEM)
@@ -259,7 +257,7 @@
     return pl.pallas_call(
         functools.partial(patch_kernel, fold, inner),
         out_shape=[jax.ShapeDtypeStruct(shape, jnp.float32) for shape in shapes],
-        in_specs=[pl.BlockSpec(memory_space=pltpu.SMEM), anywhere, vmem, vmem, vmem, vmem]
+        in_specs=[pl.BlockSpec(memory_space=pltpu.SMEM), anywhere, vmem, vmem, vmem]
         + ([] if inner else [anywhere, anywhere, vmem]),
         out_specs=[vmem] * len(shapes),
         scratch_shapes=scratch,
@@ -268,7 +266,7 @@
             flops=32 * count * length**3, bytes_accessed=16 * tile_px * tile_px, transcendentals=0
         ),
         name="patches_inner" if inner else "patches_outer",
-    )(corners, own_object, measured, probe, cosine, sine, *margins)
+    )(corners, own_object, measured, probe, fourier_parts(length), *margins)
 
 
 def fit_scalars(materials_ref, energies, kinds):

time: 130 us -> 129 us (level)
    unnamed x15 -> x13, local copies, waits for them, and re-layouts: 5.77 us -> 4.91 us
  transfers between devices with their start and end apart: 1 -> 1, of which waited for: 0 -> 0; matrix products, arithmetic and copies ran while one was open for 0% -> 0% of each run, Pallas kernels for 8% -> 11%
where the time goes in v5:
time: 129 us
  Pallas kernels  119 us (92%)
  local copies, waits for them, and re-layouts  7.49 us (6%)
  starting transfers between devices  2.44 us (2%)
    pallas_call x1, Pallas kernels, exchange_fit(): pl.pallas_call(functools.partial(exchange_kernel, groups, tiles), out_sha...  95.2 us
    pallas_call x2, Pallas kernels, patch_call(): pl.pallas_call(functools.partial(patch_kernel, fold, inner), out_shape=[j...  23.8 us
    unnamed x13, local copies, waits for them, and re-layouts  4.91 us
  transfers between devices with their start and end apart: 1, of which 0 were waited for; matrix products, arithmetic and copies ran while one was open for 0% of the time, Pallas kernels for 11%

profile of v5, /device:TPU:0, one launch (start us, length us, event | category | flops | bytes accessed | tf_op | source)
XLA Modules:
  0.0 129.0 jit_solution(561521338731181765)
XLA Ops:
  0.0 0.0 copy-start
  0.0 0.0 copy-start.5
  0.0 0.0 copy-start.4
  0.0 2.4 %slice.4 = f32[2,512,256]{2,1,0:T(8,128)} slice(f32[2,512,512]{2,1,0:T(8,128)} %bitcast.8), slice={[0:2], [0:512], [0:256]} | slice | bytes 2097152 | tf_op jit(solution)/shard_map/slice | solution.py:504
  2.4 2.4 %collective-permute-start = (f32[2,512,256]{2,1,0:T(8,128)}, f32[2,512,256]{2,1,0:T(8,128)S(1)}, u32[]{:S(2)}, u32[]{:S(2)}) collective-permute-start(f32[2,512,256]{2,1,0:T(8,128)} %slice.4), channel_id=1, source_target_pairs={{0,3},{1,0},{2,1},{3,2},{4,7},{5,4},{6,5},{7,6},{8,11},{9,8},{10,9... | collective-permute-start | bytes 3145736 | tf_op jit(solution)/shard_map/ppermute | solution.py:23
  4.9 0.0 copy-done.5
  4.9 0.1 copy.9.refs_0_
  4.9 0.0 copy-done.4
  4.9 0.1 reshape.6.materials_ref
  5.0 0.0 copy-done
  5.0 0.0 copy-start.1
  5.1 1.6 %copy-done.1 = bf16[1,1,16,256,256]{4,3,2,1,0:T(8,128)(2,1)S(1)} copy-done((bf16[1,1,16,256,256]{4,3,2,1,0:T(8,128)(2,1)S(1)}, bf16[1,1,16,256,256]{4,3,2,1,0:T(8,128)(2,1)}, u32[]{:S(2)}) %copy-start.1) | copy-done | bytes 2097176
  6.6 0.0 copy-start.2
  6.6 1.0 copy-done.2
  7.7 0.0 copy-start.3
  7.7 0.9 copy-done.3
  8.6 14.6 %patches_inner.1.refs_7_ = f32[2,6,768,128]{3,2,1,0:T(8,128)S(1)} custom-call(s32[16,2]{1,0:T(8,128)S(1)} %copy.9.refs_0_, f32[2,512,512]{2,1,0:T(8,128)S(1)} %bitcast.9, bf16[16,256,256]{2,1,0:T(8,128)(2,1)S(1)} %bitcast.11, f32[2,256,256]{2,1,0:T(8,128)S(1)} %bitcast.13, bf16[2,256,256]{2,1,0:T(8,128)(2,1)S(1)} %copy-done.3), custom_call_target="tpu_custom_call" | custom-call | flops 8589934592 | bytes 4194304 | tf_op jit(solution)/shard_map/patches_inner/pallas_call | solution.py:257
  23.2 0.0 collective-permute-done.refs_5_
  23.3 9.2 %patches_outer.1 = (f32[2,512,512]{2,1,0:T(8,128)S(1)}, f32[2,512,256]{2,1,0:T(8,128)S(1)}, f32[2,8,128]{2,1,0:T(8,128)}) custom-call(s32[16,2]{1,0:T(8,128)S(1)} %copy.9.refs_0_, f32[2,512,512]{2,1,0:T(8,128)S(1)} %bitcast.10, bf16[16,256,256]{2,1,0:T(8,128)(2,1)S(1)} %bitcast.12, f32[2,256,256]{2,1,0:T(8,128)S(1)} %bitcast.14, ...), custom_call_target="tpu_custom_call" | custom-call | flops 8589934592 | bytes 4194304 | tf_op jit(solution)/shard_map/patches_outer/pallas_call | solution.py:257
  32.4 95.2 %exchange.1 = f32[2,512,512]{2,1,0:T(8,128)S(1)} custom-call(f32[128]{0:T(128)S(1)} %reshape.6.materials_ref, f32[2,512,512]{2,1,0:T(8,128)S(1)} %get-tuple-element.7.main_ref, f32[2,512,256]{2,1,0:T(8,128)S(1)} %get-tuple-element.8.side_ref), custom_call_target="tpu_custom_call" | custom-call | tf_op jit(solution)/shard_map/exchange/pallas_call | solution.py:474
  127.7 1.3 %copy.12 = f32[1,2,1,512,512]{4,3,2,1,0:T(8,128)} copy(f32[1,2,1,512,512]{4,3,2,1,0:T(8,128)S(1)} %bitcast.7) | data formatting | bytes 4194304
  (1 shorter events, 0.0 us)
Async XLA Ops:
  0.0 5.0 %copy-start = (f32[1,2,1,512,512]{4,3,2,1,0:T(8,128)S(1)}, f32[1,2,1,512,512]{4,3,2,1,0:T(8,128)}, u32[]{:S(2)}) copy-start(f32[1,2,1,512,512]{4,3,2,1,0:T(8,128)} %param.7) | copy-start | bytes 6291460
  0.0 4.9 %copy-start.5 = (s32[1,16,2]{1,2,0:T(2,128)S(1)}, s32[1,16,2]{1,2,0:T(2,128)}, u32[]{:S(2)}) copy-start(s32[1,16,2]{1,2,0:T(2,128)} %param.10) | copy-start | bytes 388
  0.0 4.9 %copy-start.4 = (f32[2,8,8]{2,1,0:T(8,128)S(1)}, f32[2,8,8]{2,1,0:T(8,128)}, u32[]{:S(2)}) copy-start(f32[2,8,8]{2,1,0:T(8,128)} %param.11) | copy-start | bytes 1540
  2.4 20.8 %collective-permute-start = (f32[2,512,256]{2,1,0:T(8,128)}, f32[2,512,256]{2,1,0:T(8,128)S(1)}, u32[]{:S(2)}, u32[]{:S(2)}) collective-permute-start(f32[2,512,256]{2,1,0:T(8,128)} %slice.4), channel_id=1, source_target_pairs={{0,3},{1,0},{2,1},{3,2},{4,7},{5,4},{6,5},{7,6},{8,11},{9,8},{10,9... | collective-permute-start | bytes 3145736 | tf_op jit(solution)/shard_map/ppermute | solution.py:23
  5.0 1.6 %copy-start.1 = (bf16[1,1,16,256,256]{4,3,2,1,0:T(8,128)(2,1)S(1)}, bf16[1,1,16,256,256]{4,3,2,1,0:T(8,128)(2,1)}, u32[]{:S(2)}) copy-start(bf16[1,1,16,256,256]{4,3,2,1,0:T(8,128)(2,1)} %param.9) | copy-start | bytes 6291460
  6.6 1.0 copy-start.2
  7.7 0.9 copy-start.3

commit v6 on v5

--- a/solution.py
+++ b/solution.py
@@ -96,6 +96,8 @@
         ref, at = (object_ref, block) if block < blocks else (right_ref, block - blocks)
         columns = pl.ds(at * LANES, LANES)
         moves.append((ref.at[:, :, columns], field.at[:, block, top, :]))
+        if fold and not inner and block < (tile_px - length) // LANES:
+            continue
         if fold:
             source = ref.at[:, pl.ds(0, length), columns]
         elif not inner:

time: 129 us -> 129 us (level)
  transfers between devices with their start and end apart: 1 -> 1, of which waited for: 0 -> 0; matrix products, arithmetic and copies ran while one was open for 0% -> 0% of each run, Pallas kernels for 11% -> 8%
where the time goes in v6:
time: 129 us
  Pallas kernels  119 us (92%)
  local copies, waits for them, and re-layouts  7.49 us (6%)
  starting transfers between devices  2.44 us (2%)
    pallas_call x1, Pallas kernels, exchange_fit(): pl.pallas_call(functools.partial(exchange_kernel, groups, tiles), out_sha...  95.1 us
    pallas_call x2, Pallas kernels, patch_call(): pl.pallas_call(functools.partial(patch_kernel, fold, inner), out_shape=[j...  23.5 us
    unnamed x13, local copies, waits for them, and re-layouts  4.91 us
  transfers between devices with their start and end apart: 1, of which 0 were waited for; matrix products, arithmetic and copies ran while one was open for 0% of the time, Pallas kernels for 8%

profile of v6, /device:TPU:0, one launch (start us, length us, event | category | flops | bytes accessed | tf_op | source)
XLA Modules:
  0.0 128.6 jit_solution(11001190589675163680)
XLA Ops:
  0.0 0.0 copy-start
  0.0 0.0 copy-start.5
  0.0 0.0 copy-start.4
  0.0 2.4 %slice.4 = f32[2,512,256]{2,1,0:T(8,128)} slice(f32[2,512,512]{2,1,0:T(8,128)} %bitcast.8), slice={[0:2], [0:512], [0:256]} | slice | bytes 2097152 | tf_op jit(solution)/shard_map/slice | solution.py:506
  2.4 2.4 %collective-permute-start = (f32[2,512,256]{2,1,0:T(8,128)}, f32[2,512,256]{2,1,0:T(8,128)S(1)}, u32[]{:S(2)}, u32[]{:S(2)}) collective-permute-start(f32[2,512,256]{2,1,0:T(8,128)} %slice.4), channel_id=1, source_target_pairs={{0,3},{1,0},{2,1},{3,2},{4,7},{5,4},{6,5},{7,6},{8,11},{9,8},{10,9... | collective-permute-start | bytes 3145736 | tf_op jit(solution)/shard_map/ppermute | solution.py:23
  4.9 0.0 copy-done.5
  4.9 0.1 copy.9.refs_0_
  4.9 0.0 copy-done.4
  4.9 0.1 reshape.6.materials_ref
  5.0 0.0 copy-done
  5.0 0.0 copy-start.1
  5.1 1.6 %copy-done.1 = bf16[1,1,16,256,256]{4,3,2,1,0:T(8,128)(2,1)S(1)} copy-done((bf16[1,1,16,256,256]{4,3,2,1,0:T(8,128)(2,1)S(1)}, bf16[1,1,16,256,256]{4,3,2,1,0:T(8,128)(2,1)}, u32[]{:S(2)}) %copy-start.1) | copy-done | bytes 2097176
  6.6 0.0 copy-start.2
  6.6 1.0 copy-done.2
  7.7 0.0 copy-start.3
  7.7 0.9 copy-done.3
  8.6 10.1 %patches_inner.1.refs_7_ = f32[2,6,768,128]{3,2,1,0:T(8,128)S(1)} custom-call(s32[16,2]{1,0:T(8,128)S(1)} %copy.9.refs_0_, f32[2,512,512]{2,1,0:T(8,128)S(1)} %bitcast.9, bf16[16,256,256]{2,1,0:T(8,128)(2,1)S(1)} %bitcast.11, f32[2,256,256]{2,1,0:T(8,128)S(1)} %bitcast.13, bf16[2,256,256]{2,1,0:T(8,128)(2,1)S(1)} %copy-done.3), custom_call_target="tpu_custom_call" | custom-call | flops 8589934592 | bytes 4194304 | tf_op jit(solution)/shard_map/patches_inner/pallas_call | solution.py:259
  18.7 0.0 collective-permute-done.refs_5_
  18.8 13.4 %patches_outer.1 = (f32[2,512,512]{2,1,0:T(8,128)S(1)}, f32[2,512,256]{2,1,0:T(8,128)S(1)}, f32[2,8,128]{2,1,0:T(8,128)}) custom-call(s32[16,2]{1,0:T(8,128)S(1)} %copy.9.refs_0_, f32[2,512,512]{2,1,0:T(8,128)S(1)} %bitcast.10, bf16[16,256,256]{2,1,0:T(8,128)(2,1)S(1)} %bitcast.12, f32[2,256,256]{2,1,0:T(8,128)S(1)} %bitcast.14, ...), custom_call_target="tpu_custom_call" | custom-call | flops 8589934592 | bytes 4194304 | tf_op jit(solution)/shard_map/patches_outer/pallas_call | solution.py:259
  32.2 95.1 %exchange.1 = f32[2,512,512]{2,1,0:T(8,128)S(1)} custom-call(f32[128]{0:T(128)S(1)} %reshape.6.materials_ref, f32[2,512,512]{2,1,0:T(8,128)S(1)} %get-tuple-element.7.main_ref, f32[2,512,256]{2,1,0:T(8,128)S(1)} %get-tuple-element.8.side_ref), custom_call_target="tpu_custom_call" | custom-call | tf_op jit(solution)/shard_map/exchange/pallas_call | solution.py:476
  127.3 1.3 %copy.12 = f32[1,2,1,512,512]{4,3,2,1,0:T(8,128)} copy(f32[1,2,1,512,512]{4,3,2,1,0:T(8,128)S(1)} %bitcast.7) | data formatting | bytes 4194304
  (1 shorter events, 0.0 us)
Async XLA Ops:
  0.0 5.0 %copy-start = (f32[1,2,1,512,512]{4,3,2,1,0:T(8,128)S(1)}, f32[1,2,1,512,512]{4,3,2,1,0:T(8,128)}, u32[]{:S(2)}) copy-start(f32[1,2,1,512,512]{4,3,2,1,0:T(8,128)} %param.7) | copy-start | bytes 6291460
  0.0 4.9 %copy-start.5 = (s32[1,16,2]{1,2,0:T(2,128)S(1)}, s32[1,16,2]{1,2,0:T(2,128)}, u32[]{:S(2)}) copy-start(s32[1,16,2]{1,2,0:T(2,128)} %param.10) | copy-start | bytes 388
  0.0 4.9 %copy-start.4 = (f32[2,8,8]{2,1,0:T(8,128)S(1)}, f32[2,8,8]{2,1,0:T(8,128)}, u32[]{:S(2)}) copy-start(f32[2,8,8]{2,1,0:T(8,128)} %param.11) | copy-start | bytes 1540
  2.4 16.3 %collective-permute-start = (f32[2,512,256]{2,1,0:T(8,128)}, f32[2,512,256]{2,1,0:T(8,128)S(1)}, u32[]{:S(2)}, u32[]{:S(2)}) collective-permute-start(f32[2,512,256]{2,1,0:T(8,128)} %slice.4), channel_id=1, source_target_pairs={{0,3},{1,0},{2,1},{3,2},{4,7},{5,4},{6,5},{7,6},{8,11},{9,8},{10,9... | collective-permute-start | bytes 3145736 | tf_op jit(solution)/shard_map/ppermute | solution.py:23
  5.0 1.6 %copy-start.1 = (bf16[1,1,16,256,256]{4,3,2,1,0:T(8,128)(2,1)S(1)}, bf16[1,1,16,256,256]{4,3,2,1,0:T(8,128)(2,1)}, u32[]{:S(2)}) copy-start(bf16[1,1,16,256,256]{4,3,2,1,0:T(8,128)(2,1)} %param.9) | copy-start | bytes 6291460
  6.6 1.0 copy-start.2
  7.7 0.9 copy-start.3
